TPU v7x, 32 devices: a whole 2x2x4 slice. The times are simulated.
32 devices in a mesh: rows: 16 (over z, y, x), cols: 2 (over core).
Axes of the slice: x: 2, y: 2, z: 4, core: 2. Of those that a mesh axis runs over, the one named last changes fastest.
Arguments:
- row_points: float32 [3, 8192], P(None, 'rows')
- panel_points: bfloat16 [3, 512], P(None, ('rows', 'cols')), may hold values from 0 to 1
- test_vectors: bfloat16 [128, 512], P(None, ('rows', 'cols')), may hold values from -0.25 to 0.25
- leaf_skeleton: int32 [16, 64], P('rows'), may hold values from 0 to 511, as said below
- node_skeleton: int32 [16, 4, 64], P('rows'), may hold values from 0 to 127, as said below
Outputs:
- leaf_interp: float32 [64, 8192], P(None, ('rows', 'cols'))
- transfers: float32 [16, 4, 64, 128], P('rows')
- top_skeleton: float32 [16, 64, 256], P('rows')
Inputs may be any that keep to these rules, and one draw needn't show every extreme that they name: `leaf_skeleton`: each leaf's 64 entries are distinct. `node_skeleton`: each entry list holds 64 distinct positions among the 128 stacked rows (the lower child's first); all leaves under the same node have the same list at that level.
All inputs are finite; a program needn't handle non-finite values.
Results may differ from a plain program's by a relative error of at most 0.0049.
Values may be sent and summed in bfloat16 or wider, within the bound.
No kernel may reach another device: no remote copies, remote signals or barrier semaphores. Data moves between devices by JAX's collectives and lax.ppermute only.
A program may use at most 64 MiB of HBM per device.

v0:
```python
import math

import jax
import jax.numpy as jnp
from jax import lax
from jax.sharding import PartitionSpec as P

KAPPA = 40.0
SMOOTH = 0.05
RIDGE = 0.1
EPSILON = 1e-05


def from_partner(shard, axis, bit):
    return lax.ppermute(shard, axis, [(i, i ^ 1 << bit) for i in range(lax.axis_size(axis))])


def kernel_block(targets, sources):
    source_f = sources.astype(jnp.float32)
    dist_sq = jnp.zeros((targets.shape[1], source_f.shape[1]), jnp.float32)
    for component in range(3):
        offset = targets[component][:, None] - source_f[component][None, :]
        dist_sq = dist_sq + offset * offset
    radius = jnp.sqrt(dist_sq + SMOOTH * SMOOTH)
    real_part = (jnp.cos(KAPPA * radius) / radius).astype(jnp.bfloat16)
    imag_part = (jnp.sin(KAPPA * radius) / radius).astype(jnp.bfloat16)
    return (real_part, imag_part)


def sample_block(real_part, imag_part, vectors):
    first_half = jnp.dot(real_part, vectors.T, preferred_element_type=jnp.float32)
    second_half = jnp.dot(imag_part, vectors.T, preferred_element_type=jnp.float32)
    return jnp.concatenate([first_half, second_half], axis=1)


def interpolate(block, skeleton):
    gram_matrix = jnp.dot(skeleton, skeleton.T, precision=lax.Precision.HIGHEST)
    ridge = RIDGE * skeleton.shape[1] * (jnp.mean(skeleton * skeleton) + EPSILON)
    gram_matrix = gram_matrix + ridge * jnp.eye(skeleton.shape[0], dtype=jnp.float32)
    factor = jnp.linalg.cholesky(gram_matrix)
    right_side = jnp.dot(skeleton, block.T, precision=lax.Precision.HIGHEST)
    middle = lax.linalg.triangular_solve(factor, right_side, left_side=True, lower=True)
    return lax.linalg.triangular_solve(factor, middle, left_side=True, lower=True, transpose_a=True)


def body(row_points, panel_points, test_vectors, leaf_skeleton, node_skeleton):
    rows_here = row_points.shape[1]
    vec_count = test_vectors.shape[0]
    level_count = node_skeleton.shape[1]
    zero_sum = jnp.zeros((rows_here, 2 * vec_count), jnp.float32)
    running = zero_sum
    vectors = lax.all_gather(test_vectors, "rows", axis=1, tiled=True)
    sources = lax.all_gather(panel_points, "rows", axis=1, tiled=True)
    piece_width = vectors.shape[1]
    block_width = math.gcd(piece_width, 512)
    block_count = piece_width // block_width
    vec_blocks = jnp.moveaxis(vectors.reshape(vec_count, block_count, block_width), 1, 0)
    src_blocks = jnp.moveaxis(sources.reshape(3, block_count, block_width), 1, 0)

    def one_block(acc_sum, blocks):
        real_part, imag_part = kernel_block(row_points, blocks[1])
        return (acc_sum + sample_block(real_part, imag_part, blocks[0]), None)

    running, unused = lax.scan(one_block, running, (vec_blocks, src_blocks))
    half_rows = rows_here // lax.axis_size("cols")
    col_index = lax.axis_index("cols")
    samples = lax.psum(running, "cols")
    skel_rows = jnp.take(samples, leaf_skeleton[0], axis=0)
    own_samples = lax.dynamic_slice_in_dim(samples, col_index * half_rows, half_rows, 0)
    leaf_interp = interpolate(own_samples, skel_rows)
    row_index = lax.axis_index("rows")
    current = skel_rows
    level_maps = []
    for tree_level in range(level_count):
        partner = from_partner(current, "rows", tree_level)
        is_upper = jnp.right_shift(row_index, tree_level) & 1 == 1
        lower_child = jnp.where(is_upper, partner, current)
        upper_child = jnp.where(is_upper, current, partner)
        stacked = jnp.concatenate([lower_child, upper_child], axis=0)
        current = jnp.take(stacked, node_skeleton[0, tree_level], axis=0)
        level_maps.append(interpolate(stacked, current))
    path_maps = jnp.stack(level_maps)
    return (leaf_interp, path_maps[None], current[None])


def solution(mesh):
    placed = (
        P(None, "rows"),
        P(None, ("rows", "cols")),
        P(None, ("rows", "cols")),
        P("rows", None),
        P("rows", None, None),
    )
    return jax.shard_map(
        body,
        mesh=mesh,
        in_specs=placed,
        out_specs=(P(None, ("rows", "cols")), P("rows", None, None, None), P("rows", None, None)),
        check_vma=False,
    )
```

profile of v0, /device:TPU:1, one launch (start us, length us, event | category | flops | bytes accessed | tf_op | source)
XLA Modules:
  0.0 201.7 jit_solution(5670295947467593674)
XLA Ops:
  7.8 34.6 %all-gather = bf16[16,16,3]{1,2,0:T(4,128)(2,1)S(1)} all-gather(bf16[1,16,3]{1,2,0:T(4,128)(2,1)S(1)} %bitcast.136), channel_id=1, replica_groups=mesh['rows'=16,'cols'=2] {'rows'}, dimensions={0}, use_global_device_ids=true | all-gather | bytes 1632 | tf_op jit(solution)/shard_map/all_gather | solution.py:53
  43.1 0.7 copy-done.2
  43.8 28.8 %all_gather.7 = bf16[128,256]{0,1:T(8,128)(2,1)S(1)} all-gather(bf16[128,16]{0,1:T(8,128)(2,1)S(1)} %copy-done.2), channel_id=1, replica_groups=mesh['rows'=16,'cols'=2] {'rows'}, dimensions={1}, use_global_device_ids=true | all-gather | bytes 69632 | tf_op jit(solution)/shard_map/all_gather | solution.py:52
  72.6 2.4 %fusion = f32[512,128]{0,1:T(8,128)S(1)} fusion(bf16[128,256]{0,1:T(8,128)(2,1)S(1)} %all_gather.7, f32[256]{0:T(256)S(1)} %bitcast.139, f32[512]{0:T(512)S(1)} %bitcast.132, f32[256]{0:T(256)S(1)} %bitcast.141, f32[512]{0:T(512)S(1)} %bitcast.134, f32[256]{0:T(256)S(1)} %bitcast.137, f32[512]{0:T(512)S(1)} %bitcast.130), kind=kOutput, calls=%fused_computation.18 | convolution fusion | flops 35127296 | bytes 336896 | tf_op jit(solution)/shard_map/while/body/eval_jaxpr/dot_general | solution.py:31
  75.0 2.4 %fusion.1 = f32[512,128]{0,1:T(8,128)S(1)} fusion(bf16[128,256]{0,1:T(8,128)(2,1)S(1)} %all_gather.7, f32[256]{0:T(256)S(1)} %bitcast.140, f32[512]{0:T(512)S(1)} %bitcast.133, f32[256]{0:T(256)S(1)} %bitcast.142, f32[512]{0:T(512)S(1)} %bitcast.135, f32[256]{0:T(256)S(1)} %bitcast.138, f32[512]{0:T(512)S(1)} %bitcast.131), kind=kOutput, calls=%fused_computation.19 | convolution fusion | flops 35127296 | bytes 336896 | tf_op jit(solution)/shard_map/while/body/eval_jaxpr/dot_general | solution.py:32
  77.4 0.8 pad_maximum_fusion
  79.0 0.7 copy-done.3
  79.8 29.7 %all-reduce.2.cloned.1.call-done = f32[512,256]{0,1:T(8,128)} async-done(((f32[512,256]{0,1:T(8,128)}), f32[512,256]{0,1:T(8,128)}) %all-reduce.2.cloned.1.call-update) | async-done | bytes 524304 | tf_op jit(solution)/shard_map/psum | solution.py:67
  109.4 1.2 copy.53
  110.7 0.7 gather_fusion
  111.3 0.7 multiply_reduce_fusion.4
  112.0 1.5 collective-permute-start
  114.5 5.8 %cholesky.89 = f32[64,64]{1,0:T(8,128)S(1)} custom-call(f32[64,64]{1,0:T(8,128)S(1)} %fusion.48), custom_call_target="Cholesky" | custom-call | tf_op jit(solution)/shard_map/jit(cholesky)/cholesky | solution.py:40
  121.9 4.9 %custom-call.13 = f32[1,64,64]{1,2,0:T(8,128)S(1)} custom-call(f32[1,64,64]{2,1,0:T(8,128)S(1)} %copy.58), custom_call_target="InvertDiagBlocksLowerTriangular" | custom-call | tf_op jit(solution)/shard_map/triangular_solve | solution.py:43
  127.4 0.8 fusion.44
  128.9 0.7 multiply_reduce_fusion.3
  129.9 1.3 collective-permute-start.1
  132.1 5.8 %cholesky.100 = f32[64,64]{1,0:T(8,128)S(1)} custom-call(f32[64,64]{1,0:T(8,128)S(1)} %fusion.43), custom_call_target="Cholesky" | custom-call | tf_op jit(solution)/shard_map/jit(cholesky)/cholesky | solution.py:40
  139.3 4.9 %custom-call.21 = f32[1,64,64]{1,2,0:T(8,128)S(1)} custom-call(f32[1,64,64]{2,1,0:T(8,128)S(1)} %fusion.24), custom_call_target="InvertDiagBlocksLowerTriangular" | custom-call | tf_op jit(solution)/shard_map/triangular_solve/custom-call.4 | solution.py:43
  145.3 0.7 multiply_reduce_fusion.2
  146.2 1.3 collective-permute-start.2
  148.5 5.8 %cholesky.111 = f32[64,64]{1,0:T(8,128)S(1)} custom-call(f32[64,64]{1,0:T(8,128)S(1)} %fusion.39), custom_call_target="Cholesky" | custom-call | tf_op jit(solution)/shard_map/jit(cholesky)/cholesky | solution.py:40
  155.7 4.9 %custom-call.23 = f32[1,64,64]{1,2,0:T(8,128)S(1)} custom-call(f32[1,64,64]{2,1,0:T(8,128)S(1)} %fusion.25), custom_call_target="InvertDiagBlocksLowerTriangular" | custom-call | tf_op jit(solution)/shard_map/triangular_solve/custom-call.4 | solution.py:43
  161.7 0.7 multiply_reduce_fusion.1
  162.6 2.2 %collective-permute-start.3 = (f32[64,256]{1,0:T(8,128)S(1)}, f32[64,256]{1,0:T(8,128)S(1)}, u32[]{:S(2)}, u32[]{:S(2)}) collective-permute-start(f32[64,256]{1,0:T(8,128)S(1)} %get-tuple-element.27), channel_id=1, source_target_pairs={{0,16},{2,18},{4,20},{6,22},{8,24},{10,26},{12,28},{14,30},{16,0},... | collective-permute-start | bytes 196616 | tf_op jit(solution)/shard_map/ppermute | solution.py:15
  165.8 5.8 %cholesky.122 = f32[64,64]{1,0:T(8,128)S(1)} custom-call(f32[64,64]{1,0:T(8,128)S(1)} %fusion.35), custom_call_target="Cholesky" | custom-call | tf_op jit(solution)/shard_map/jit(cholesky)/cholesky | solution.py:40
  173.0 4.9 %custom-call.25 = f32[1,64,64]{1,2,0:T(8,128)S(1)} custom-call(f32[1,64,64]{2,1,0:T(8,128)S(1)} %fusion.26), custom_call_target="InvertDiagBlocksLowerTriangular" | custom-call | tf_op jit(solution)/shard_map/triangular_solve/custom-call.4 | solution.py:43
  178.4 0.7 gather_fusion.4
  179.0 1.3 select_bitcast_fusion
  181.7 5.8 %cholesky.133 = f32[64,64]{1,0:T(8,128)S(1)} custom-call(f32[64,64]{1,0:T(8,128)S(1)} %fusion.31), custom_call_target="Cholesky" | custom-call | tf_op jit(solution)/shard_map/jit(cholesky)/cholesky | solution.py:40
  188.8 4.9 %custom-call.27 = f32[1,64,64]{1,2,0:T(8,128)S(1)} custom-call(f32[1,64,64]{2,1,0:T(8,128)S(1)} %fusion.27), custom_call_target="InvertDiagBlocksLowerTriangular" | custom-call | tf_op jit(solution)/shard_map/triangular_solve/custom-call.4 | solution.py:43
  194.2 0.7 maximum_bitcast_fusion
  (85 shorter events, 15.8 us)
Async XLA Ops:
  7.2 0.7 copy-start.4
  7.2 102.2 %all-reduce.2.cloned.1.call-start = ((), (), s32[]{:S(2)}) async-start(), calls=%async_computation | async-start | bytes 1048576 | tf_op jit(solution)/shard_map/psum | solution.py:67
  42.4 0.7 copy-start.1
  43.1 0.7 copy-start.2
  78.3 0.7 copy-start.5
  79.0 0.7 copy-start.3
  110.7 16.2 %copy-start = (f32[512,256]{0,1:T(8,128)S(1)}, f32[512,256]{0,1:T(8,128)}, u32[]{:S(2)}) copy-start(f32[512,256]{0,1:T(8,128)} %all-reduce.2.cloned.1.call-done) | copy-start | bytes 1572868
  112.0 16.2 %collective-permute-start = (f32[64,256]{1,0:T(8,128)S(1)}, f32[64,256]{1,0:T(8,128)S(1)}, u32[]{:S(2)}, u32[]{:S(2)}) collective-permute-start(f32[64,256]{1,0:T(8,128)S(1)} %get-tuple-element.37), channel_id=1, source_target_pairs={{0,2},{2,0},{4,6},{6,4},{8,10},{10,8},{12,14},{14,12},{16,18},{18,... | collective-permute-start | bytes 196616 | tf_op jit(solution)/shard_map/ppermute | solution.py:15
  129.9 14.7 %collective-permute-start.1 = (f32[64,256]{1,0:T(8,128)S(1)}, f32[64,256]{1,0:T(8,128)S(1)}, u32[]{:S(2)}, u32[]{:S(2)}) collective-permute-start(f32[64,256]{1,0:T(8,128)S(1)} %get-tuple-element.23), channel_id=1, source_target_pairs={{0,4},{2,6},{4,0},{6,2},{8,12},{10,14},{12,8},{14,10},{16,20},{18,... | collective-permute-start | bytes 196616 | tf_op jit(solution)/shard_map/ppermute | solution.py:15
  146.2 14.7 %collective-permute-start.2 = (f32[64,256]{1,0:T(8,128)S(1)}, f32[64,256]{1,0:T(8,128)S(1)}, u32[]{:S(2)}, u32[]{:S(2)}) collective-permute-start(f32[64,256]{1,0:T(8,128)S(1)} %get-tuple-element.25), channel_id=1, source_target_pairs={{0,8},{2,10},{4,12},{6,14},{8,0},{10,2},{12,4},{14,6},{16,24},{18,... | collective-permute-start | bytes 196616 | tf_op jit(solution)/shard_map/ppermute | solution.py:15
  162.6 15.7 %collective-permute-start.3 = (f32[64,256]{1,0:T(8,128)S(1)}, f32[64,256]{1,0:T(8,128)S(1)}, u32[]{:S(2)}, u32[]{:S(2)}) collective-permute-start(f32[64,256]{1,0:T(8,128)S(1)} %get-tuple-element.27), channel_id=1, source_target_pairs={{0,16},{2,18},{4,20},{6,22},{8,24},{10,26},{12,28},{14,30},{16,0},... | collective-permute-start | bytes 196616 | tf_op jit(solution)/shard_map/ppermute | solution.py:15
Sparse Core Ops, SparseCore 0:
  78.4 30.9 all-reduce.1
where the time goes:
time: 203 us; the launch traced here: 202 us
  other arithmetic  66.2 us (33%)
  blocking collectives  63.4 us (31%)
  waiting for transfers between devices  29.7 us (15%)
  between operations  17.8 us (9%)
  matrix products  9.95 us (5%)
  local copies, waits for them, and re-layouts  8.37 us (4%)
  starting transfers between devices  6.25 us (3%)
    all_gather x1, blocking collectives, body(): sources = lax.all_gather(panel_points, 'rows', axis=1, tiled=True)  34.6 us
    another operation x15, other arithmetic, interpolate(): factor = jnp.linalg.cholesky(gram_matrix)  32.7 us
    psum x1, waiting for transfers between devices, body(): samples = lax.psum(running, 'cols')  29.7 us
    all_gather x1, blocking collectives, body(): vectors = lax.all_gather(test_vectors, 'rows', axis=1, tiled=True)  28.8 us
    another operation x10, other arithmetic, interpolate(): lax.linalg.triangular_solve(factor, middle, left_side=True, lower=True, t...  27.8 us
    ppermute x4, starting transfers between devices, from_partner(): lax.ppermute(shard, axis, [(i, i ^ 1 << bit) for i in range(lax.axis_size...  6.21 us
  transfers between devices with their start and end apart: 5, of which 1 were waited for; matrix products, arithmetic and copies ran while one was open for 26% of the time, Pallas kernels for 0%

commit v1 on v0

v1 whole, which is shorter than its diff:
```python
import functools
import math

import jax
import jax.numpy as jnp
from jax import lax
from jax.experimental import pallas as pl
from jax.experimental.pallas import tpu as pltpu
from jax.sharding import PartitionSpec as P

KAPPA = 40.0
SMOOTH = 0.05
RIDGE = 0.1
EPSILON = 1e-05

LANES = 128
SUB = 8
VMEM = pl.BlockSpec(memory_space=pltpu.VMEM)

SIN_POLY = (4.442882834144944, -7.308241154366058, 3.606288956137823, -0.8457635864795654, 0.10920573808065867)
COS_POLY = (1.4142134965650128, -6.978850988238946, 5.739461170681512, -1.8835629873012505, 0.31069819181076774)


def iota(shape, dim):
    return lax.broadcasted_iota(jnp.int32, shape, dim)


def take_lanes(x, index):
    return jnp.take_along_axis(x, index, axis=1)


def swap_halves(x):
    return pltpu.roll(x, LANES // 2, axis=1)


def mm(a, b, dims=((1,), (0,)), precision=None):
    return lax.dot_general(a, b, (dims, ((), ())), precision=precision, preferred_element_type=jnp.float32)


def mm_exact(a, b):
    return mm(a, b, precision=lax.Precision.HIGHEST)


def split3(x):
    high = x.astype(jnp.bfloat16).astype(jnp.float32)
    rest = x - high
    mid = rest.astype(jnp.bfloat16).astype(jnp.float32)
    return high, mid, rest - mid


def pack_kernel(rows_ref, points_ref, vectors_ref, leaf_ref, node_ref, out_ref, stage):
    width = vectors_ref.shape[1]
    half = LANES // 2
    low = iota((1, LANES), 1) < half
    stage[...] = jnp.zeros_like(stage)
    stage[0:1, 0:half] = leaf_ref[...].astype(jnp.float32)
    stage[1:5, 0:half] = node_ref[0].astype(jnp.float32)
    stage[5:8, 0:width] = points_ref[...].astype(jnp.float32)
    s = stage[...]
    index = s[0:1]
    index = (index + swap_halves(jnp.broadcast_to(index, (SUB, LANES)))[0:1]).astype(jnp.int32)
    index = jnp.broadcast_to(index, (SUB, LANES))
    stage[0:3, :] = rows_ref[:, 0:LANES]
    found = jnp.zeros((SUB, LANES), jnp.float32)
    for tile in range(rows_ref.shape[1] // LANES):
        stage[0:3, :] = rows_ref[:, tile * LANES : (tile + 1) * LANES]
        picked = take_lanes(stage[...], index & (LANES - 1))
        found = jnp.where(index // LANES == tile, picked, found)
    high, mid, tail = split3(found)
    swapped = swap_halves(s)
    lines = [
        jnp.where(low, high[0:1], mid[0:1]),
        jnp.where(low, tail[0:1], high[1:2]),
        jnp.where(low, mid[1:2], tail[1:2]),
        jnp.where(low, high[2:3], mid[2:3]),
        tail[2:3],
        jnp.where(low, s[1:2], swapped[2:3]),
        jnp.where(low, s[3:4], swapped[4:5]),
        s[5:6] + pltpu.roll(s, width, axis=1)[6:7] + pltpu.roll(s, 2 * width, axis=1)[7:8],
    ]
    eye = (iota((width, width), 0) == iota((width, width), 1)).astype(jnp.bfloat16)
    columns = mm(eye, vectors_ref[...], dims=((1,), (1,)))
    block = jnp.concatenate([columns] + lines, axis=0).astype(jnp.bfloat16)

    def put(device, unused):
        out_ref[device] = block
        return unused

    lax.fori_loop(0, out_ref.shape[0], put, 0)


def main_kernel(levels, got_ref, rows_ref, node_ref, interp_ref, maps_ref, top_ref, stage, kre_ref, kim_ref, samples_ref):
    half = LANES // 2
    leaf = lax.axis_index("rows")
    column = lax.axis_index("cols")
    cols = lax.axis_size("cols")
    group_leaves = 2**levels
    group_devices = group_leaves * cols
    devices = got_ref.shape[0]
    width = got_ref.shape[1] - SUB
    lane8 = iota((SUB, LANES), 1)
    sub8 = iota((SUB, LANES), 0)
    low8 = lane8 < half
    member = leaf % group_leaves
    mine = sub8 == member // 2

    group_start = (leaf // group_leaves) * group_devices
    extra = got_ref[pl.ds(group_start, group_devices), width : width + SUB, :].astype(jnp.float32)
    extra = extra.reshape(group_devices * SUB, LANES).astype(jnp.bfloat16)
    shape = (7 * 16, group_devices * SUB)
    at = iota(shape, 0)
    source = ((at % 8) * 2 + (at // 8) % 2) * (cols * SUB) + at // 16
    picked = mm((iota(shape, 1) == source).astype(jnp.bfloat16), extra)
    even = [picked[r * 16 : r * 16 + 8] for r in range(7)]
    odd = [picked[r * 16 + 8 : r * 16 + 16] for r in range(7)]
    even_s = [swap_halves(v) for v in even]
    odd_s = [swap_halves(v) for v in odd]
    coords = [
        jnp.where(low8, even[0] + even_s[0] + even[1], odd[0] + odd_s[0] + odd_s[1]),
        jnp.where(low8, even_s[1] + (even[2] + even_s[2]), odd[1] + (odd[2] + odd_s[2])),
        jnp.where(low8, even[3] + even_s[3] + even[4], odd[3] + odd_s[3] + odd[4]),
    ]
    lists = [
        jnp.where(low8, even[5], even_s[5]).astype(jnp.int32),
        jnp.where(low8, even_s[5], even[5]).astype(jnp.int32),
        jnp.where(low8, even[6], even_s[6]).astype(jnp.int32),
        jnp.where(low8, even_s[6], even[6]).astype(jnp.int32),
    ]

    def own_row(x):
        return jnp.sum(jnp.where(mine, x, jnp.zeros_like(x)), axis=0, keepdims=True)

    siblings = []
    own_lists = [own_row(lists[0])]
    stacked = coords
    for level in range(1, levels):
        own = [take_lanes(v, lists[level - 1]) for v in stacked]
        step = 2 ** (level - 1)
        upper = (sub8 // step) % 2 == 1
        other = [jnp.where(upper, pltpu.roll(v, step, axis=0), pltpu.roll(v, SUB - step, axis=0)) for v in own]
        siblings.append([own_row(v) for v in other])
        stacked = [jnp.where(low8 == upper, b, a) for a, b in zip(own, other)]
        own_lists.append(own_row(lists[level]))
    low1 = iota((1, LANES), 1) < half
    tiles = [[own_row(v) for v in coords]]
    tiles.append([jnp.where(low1, a, b) for a, b in zip(siblings[0], siblings[1])])
    tiles.append(siblings[2])
    own_rows = rows_ref.shape[1] // cols
    own_tiles = own_rows // LANES
    start = pl.multiple_of(column * own_rows, LANES)
    own_points = rows_ref[:, pl.ds(start, own_rows)]
    for tile in range(own_tiles):
        part = own_points[:, tile * LANES : (tile + 1) * LANES]
        tiles.append([part[c : c + 1] for c in range(3)])
    total = len(tiles) * LANES

    block_devices = min(devices, group_devices)
    block = block_devices * width
    vec_count = got_ref.shape[2]
    eye = (iota((vec_count, vec_count), 0) == iota((vec_count, vec_count), 1)).astype(jnp.bfloat16)
    shape = (block, block_devices * SUB)
    spread = (iota(shape, 1) == (iota(shape, 0) // width) * SUB + SUB - 1).astype(jnp.bfloat16)
    shape = (block, LANES)
    keep = ((iota(shape, 1) % width) == (iota(shape, 0) % width)) & (iota(shape, 1) < 3 * width)
    shape = (LANES, 3 * LANES)
    collect = (iota(shape, 0) // width == iota(shape, 1) // LANES).astype(jnp.bfloat16)

    def panel_block(number, first):
        got = got_ref[pl.ds(number * block_devices, block_devices)].astype(jnp.float32)
        vectors = got[:, 0:width, :].reshape(block, vec_count).astype(jnp.bfloat16)
        tail = got[:, width : width + SUB, :].reshape(block_devices * SUB, LANES).astype(jnp.bfloat16)
        points = mm(spread, tail)
        points = jnp.where(keep, points, 0.0).astype(jnp.bfloat16)
        points = mm(points, collect)
        stage_p = [points[:, c * LANES : (c + 1) * LANES] for c in range(3)]
        for tile, target in enumerate(tiles):
            for at in range(0, block, 16):
                dist = jnp.full((16, LANES), SMOOTH * SMOOTH, jnp.float32)
                for c in range(3):
                    offset = target[c] - stage_p[c][at : at + 16]
                    dist = dist + offset * offset
                inverse = lax.rsqrt(dist)
                turns = (dist * inverse) * (KAPPA / (2 * math.pi))
                f = turns - jnp.round(turns)
                u = f * f
                sine = SIN_POLY[4]
                cosine = COS_POLY[4]
                for degree in (3, 2, 1, 0):
                    sine = sine * u + SIN_POLY[degree]
                    cosine = cosine * u + COS_POLY[degree]
                sine = sine * f
                real = (1.0 - sine * sine) * inverse
                imag = (sine * cosine) * inverse
                kre_ref[at : at + 16, tile * LANES : (tile + 1) * LANES] = real.astype(jnp.bfloat16)
                kim_ref[at : at + 16, tile * LANES : (tile + 1) * LANES] = imag.astype(jnp.bfloat16)
        vectors = mm(eye, vectors, dims=((1,), (1,))).astype(jnp.bfloat16)
        new_re = mm(vectors, kre_ref[...])
        new_im = mm(vectors, kim_ref[...])
        if first:
            samples_ref[0:vec_count, :] = new_re
            samples_ref[vec_count : 2 * vec_count, :] = new_im
        else:
            samples_ref[0:vec_count, :] += new_re
            samples_ref[vec_count : 2 * vec_count, :] += new_im

    panel_block(0, True)
    if devices > block_devices:

        def more(number, unused):
            panel_block(number, False)
            return unused

        lax.fori_loop(1, devices // block_devices, more, 0)

    full = (2 * vec_count, LANES)
    low = iota(full, 1) < half
    pair0 = samples_ref[:, 0:LANES]
    pair12 = samples_ref[:, LANES : 2 * LANES]
    pair12_s = swap_halves(pair12)
    pair3 = samples_ref[:, 2 * LANES : 3 * LANES]

    def is_upper(level):
        return ((iota(full, 0) * 0 + member) // 2**level) % 2 == 1

    stacks = [pair0]
    skels = [jnp.where(is_upper(0) == low, swap_halves(pair0), pair0)]
    skels_full = []
    for level in range(levels):
        picked = take_lanes(stacks[level], jnp.broadcast_to(own_lists[level], full))
        skels_full.append(picked)
        if level + 1 < levels:
            up = is_upper(level + 1)
            if level == 0:
                other = jnp.where(up, pair12, pair12_s)
            elif level == 1:
                other = jnp.where(up, pair12_s, pair12)
            else:
                other = pair3
            stacks.append(jnp.where(low == up, other, picked))
    own0 = jnp.where(is_upper(0), swap_halves(pair0), pair0)
    own0 = jnp.where(low, own0, swap_halves(own0))
    skels = [own0] + skels_full

    def rows_of(a, b):
        return jnp.where(low, a, b).T

    two = [rows_of(skels[0], skels[1]), rows_of(skels[2], skels[3]), rows_of(skels[4], skels[4])]
    row_form = [two[0][0:half], two[0][half:], two[1][0:half], two[1][half:], two[2][0:half]]
    top_ref[0] = row_form[4]

    right_leaf = mm_exact(row_form[0], samples_ref[:, 3 * LANES : (3 + own_tiles) * LANES])
    right_maps = [mm_exact(row_form[level + 1], stacks[level]) for level in range(levels)]
    square = (half, LANES)
    low64 = iota(square, 1) < half
    grams = [mm_exact(row_form[0], skels[0])]
    for level in range(levels):
        grams.append(take_lanes(right_maps[level], jnp.broadcast_to(own_lists[level], square)))
    pairs = []
    diagonal = iota(square, 0) == iota(square, 1) % half
    for a, b in ((0, 1), (2, 3), (4, 4)):
        gram = jnp.where(low64, grams[a], grams[b])
        trace = jnp.sum(jnp.where(diagonal, gram, 0.0), axis=0, keepdims=True)
        first = jnp.sum(jnp.where(low1, trace, 0.0), axis=1, keepdims=True)
        second = jnp.sum(jnp.where(low1, 0.0, trace), axis=1, keepdims=True)
        trace = jnp.where(low1, first, second)
        ridge = RIDGE * (2 * vec_count) * (trace * (1.0 / (half * 2 * vec_count)) + EPSILON)
        gram = gram + jnp.where(diagonal, ridge, 0.0)
        pairs.append([gram[r * SUB : (r + 1) * SUB] for r in range(half // SUB)])

    where_in_half = lane8 % half
    half_base = lane8 - where_in_half

    def eliminate(turn, blocks):
        out = [list(b) for b in blocks]
        for s in range(SUB):
            pivot_at = turn * SUB + s
            index = half_base + pivot_at
            here = where_in_half == pivot_at
            for n in range(len(out)):
                a = out[n]
                column_of = [take_lanes(v, index) for v in a]
                pivot = jnp.broadcast_to(column_of[0][s : s + 1], (SUB, LANES))
                line = jnp.broadcast_to(a[0][s : s + 1], (SUB, LANES))
                line = jnp.where(here, 1.0, line) * (1.0 / pivot)
                a = [jnp.where(here, 0.0, v) - c * line for v, c in zip(a, column_of)]
                a[0] = jnp.where(sub8 == s, line, a[0])
                out[n] = a
        return tuple(tuple(b[1:] + b[:1]) for b in out)

    done = lax.fori_loop(0, half // SUB, eliminate, tuple(tuple(b) for b in pairs))
    inverse = [jnp.concatenate(list(b), axis=0) for b in done]

    zero = jnp.zeros((half, LANES), jnp.float32)
    wide = jnp.zeros((half, own_rows), jnp.float32)
    result = mm_exact(
        inverse[0],
        jnp.concatenate(
            [jnp.concatenate([right_leaf, zero], axis=1), jnp.concatenate([wide, right_maps[0]], axis=1)], axis=0
        ),
    )
    interp_ref[...] = result[:, 0:own_rows]
    maps_ref[0, 0] = result[:, own_rows:]
    result = mm_exact(
        inverse[1],
        jnp.concatenate(
            [jnp.concatenate([right_maps[1], zero], axis=1), jnp.concatenate([zero, right_maps[2]], axis=1)], axis=0
        ),
    )
    maps_ref[0, 1] = result[:, 0:LANES]
    maps_ref[0, 2] = result[:, LANES:]
    maps_ref[0, 3] = mm_exact(inverse[2], jnp.concatenate([right_maps[3], zero], axis=0))


def body(row_points, panel_points, test_vectors, leaf_skeleton, node_skeleton):
    devices = lax.axis_size("rows") * lax.axis_size("cols")
    vec_count, width = test_vectors.shape
    rows_here = row_points.shape[1]
    levels, skel = node_skeleton.shape[1:]
    packed = pl.pallas_call(
        pack_kernel,
        out_shape=jax.ShapeDtypeStruct((devices, width + SUB, vec_count), jnp.bfloat16),
        in_specs=[VMEM] * 5,
        out_specs=VMEM,
        scratch_shapes=[pltpu.VMEM((SUB, LANES), jnp.float32)],
    )(row_points, panel_points, test_vectors, leaf_skeleton, node_skeleton)
    got = lax.all_to_all(packed, ("rows", "cols"), 0, 0, tiled=True)
    own_rows = rows_here // lax.axis_size("cols")
    lanes = 3 * LANES + own_rows
    block = min(devices, 2**levels * lax.axis_size("cols")) * width
    return pl.pallas_call(
        functools.partial(main_kernel, levels),
        out_shape=(
            jax.ShapeDtypeStruct((skel, own_rows), jnp.float32),
            jax.ShapeDtypeStruct((1, levels, skel, 2 * skel), jnp.float32),
            jax.ShapeDtypeStruct((1, skel, 2 * vec_count), jnp.float32),
        ),
        in_specs=[VMEM] * 3,
        out_specs=(VMEM, VMEM, VMEM),
        scratch_shapes=[
            pltpu.VMEM((SUB, LANES), jnp.float32),
            pltpu.VMEM((block, lanes), jnp.bfloat16),
            pltpu.VMEM((block, lanes), jnp.bfloat16),
            pltpu.VMEM((2 * vec_count, lanes), jnp.float32),
        ],
    )(got, row_points, node_skeleton)


def solution(mesh):
    placed = (
        P(None, "rows"),
        P(None, ("rows", "cols")),
        P(None, ("rows", "cols")),
        P("rows", None),
        P("rows", None, None),
    )
    return jax.shard_map(
        body,
        mesh=mesh,
        in_specs=placed,
        out_specs=(P(None, ("rows", "cols")), P("rows", None, None, None), P("rows", None, None)),
        check_vma=False,
    )
```

time: 203 us -> 31.3 us (0.15)
  other arithmetic: 66.2 us -> 0 us
  blocking collectives: 63.4 us -> 16.4 us
  waiting for transfers between devices: 29.7 us -> 0 us
  between operations: 17.8 us -> 0.63 us
  Pallas kernels: 0 us -> 12.5 us
  matrix products: 9.95 us -> 0 us
  local copies, waits for them, and re-layouts: 8.37 us -> 1.4 us
  starting transfers between devices: 6.25 us -> 0 us
    all_gather x2 -> x0, blocking collectives: 63.4 us -> none  [the longest x1 34.6 us: body(): sources = lax.all_gather(panel_points, 'rows', axis=1, tiled=True)]
    another operation x25 -> x0, other arithmetic: 60.4 us -> none  [the longest x15 32.7 us: interpolate(): factor = jnp.linalg.cholesky(gram_matrix)]
    psum x1 -> x0, waiting for transfers between devices: 29.7 us -> none  [body(): samples = lax.psum(running, 'cols')]
    all_to_all x0 -> x1, blocking collectives: none -> 16.4 us  [body(): got = lax.all_to_all(packed, ('rows', 'cols'), 0, 0, tiled=True)]
    pallas_call x0 -> x2, Pallas kernels: none -> 12.5 us  [the longest x1 10.7 us: body(): pl.pallas_call(functools.partial(main_kernel, levels), out_shape=(jax.Sha...]
    dot_general x12 -> x0, matrix products: 7.21 us -> none  [the longest x1 2.39 us: sample_block(): jnp.dot(imag_part, vectors.T, preferred_element_type=jnp.float32)]
    ppermute x4 -> x0, starting transfers between devices: 6.21 us -> none  [from_partner(): lax.ppermute(shard, axis, [(i, i ^ 1 << bit) for i in range(lax.axis_size...]
    gather x5 -> x0, local copies, waits for them, and re-layouts: 3.27 us -> none  [the longest x4 2.62 us: body(): current = jnp.take(stacked, node_skeleton[0, tree_level], axis=0)]
  transfers between devices with their start and end apart: 5 -> 0, of which waited for: 1 -> 0; matrix products, arithmetic and copies ran while one was open for 26% -> 0% of each run, Pallas kernels for 0% -> 0%
where the time goes in v1:
time: 31.3 us; the launch traced here: 31 us
  blocking collectives  16.4 us (52%)
  Pallas kernels  12.5 us (40%)
  local copies, waits for them, and re-layouts  1.4 us (4%)
  between operations  0.63 us (2%)
    all_to_all x1, blocking collectives, body(): got = lax.all_to_all(packed, ('rows', 'cols'), 0, 0, tiled=True)  16.4 us
    pallas_call x1, Pallas kernels, body(): pl.pallas_call(functools.partial(main_kernel, levels), out_shape=(jax.Sha...  10.7 us
    pallas_call x1, Pallas kernels, body(): pl.pallas_call(pack_kernel, out_shape=jax.ShapeDtypeStruct((devices, widt...  1.83 us
    unnamed x1, local copies, waits for them, and re-layouts  1.4 us

profile of v1, /device:TPU:1, one launch (start us, length us, event | category | flops | bytes accessed | tf_op | source)
XLA Modules:
  0.0 31.0 jit_solution(4563083198788088255)
XLA Ops:
  0.6 1.4 %copy.8.vectors_ref = bf16[128,16]{1,0:T(8,128)(2,1)} copy(bf16[128,16]{0,1:T(8,128)(2,1)} %param.7) | data formatting | bytes 8192 | tf_op args[2]
  2.0 1.8 %shard_map.76 = bf16[32,24,128]{2,1,0:T(8,128)(2,1)} custom-call(f32[3,512]{1,0:T(4,128)} %rows_ref.3, bf16[3,16]{1,0:T(4,128)(2,1)} %points_ref.1, bf16[128,16]{1,0:T(8,128)(2,1)} %copy.8.vectors_ref, s32[1,64]{1,0:T(1,128)} %leaf_ref.1, s32[1,4,64]{2,1,0:T(4,128)} %node_ref.3), custom_call_target="tpu_custom_call" | custom-call | tf_op jit(solution)/shard_map/pallas_call | solution.py:319
  3.9 16.4 %all_to_all.5.got_ref = bf16[32,24,128]{2,1,0:T(8,128)(2,1)} all-to-all(bf16[32,24,128]{2,1,0:T(8,128)(2,1)} %shard_map.76), channel_id=1, replica_groups=mesh['rows'=16,'cols'=2] {'rows','cols'}, dimensions={0} | all-to-all | bytes 393216 | tf_op jit(solution)/shard_map/all_to_all | solution.py:326
  20.3 10.7 %shard_map.77 = (f32[64,256]{1,0:T(8,128)}, f32[1,4,64,128]{3,2,1,0:T(8,128)}, f32[1,64,256]{2,1,0:T(8,128)}) custom-call(bf16[32,24,128]{2,1,0:T(8,128)(2,1)} %all_to_all.5.got_ref, f32[3,512]{1,0:T(4,128)} %rows_ref.3, s32[1,4,64]{2,1,0:T(4,128)} %node_ref.3), custom_call_target="tpu_custom_call" | custom-call | tf_op jit(solution)/shard_map/pallas_call | solution.py:330

commit v2 on v1

v2 whole, which is shorter than its diff:
```python
import functools
import math

import jax
import jax.numpy as jnp
import numpy as np
from jax import lax
from jax.experimental import pallas as pl
from jax.experimental.pallas import tpu as pltpu
from jax.sharding import PartitionSpec as P

KAPPA = 40.0
SMOOTH = 0.05
RIDGE = 0.1
EPSILON = 1e-05

LANES = 128
SUB = 8
VMEM = pl.BlockSpec(memory_space=pltpu.VMEM)

TURNS = KAPPA / (2 * math.pi)
SIN_POLY = (4.442867902871973, -7.30744341774541, 3.594788055359915, -0.7843739844598376)
COS_POLY = (1.4142134965650128, -6.978850988238946, 5.739461170681512, -1.8835629873012505, 0.31069819181076774)


def bf16_parts(value):
    parts = []
    for unused in range(3):
        parts.append(float(np.float32(value).astype(jnp.bfloat16)))
        value -= parts[-1]
    return parts


SCALE_PARTS = bf16_parts(TURNS * TURNS)


def iota(shape, dim):
    return lax.broadcasted_iota(jnp.int32, shape, dim)


def take_lanes(x, index):
    return jnp.take_along_axis(x, index, axis=1)


def swap_halves(x):
    return pltpu.roll(x, LANES // 2, axis=1)


def mm(a, b, dims=((1,), (0,)), precision=None):
    return lax.dot_general(a, b, (dims, ((), ())), precision=precision, preferred_element_type=jnp.float32)


def split2(x):
    high = x.astype(jnp.bfloat16)
    return high, (x - high.astype(jnp.float32)).astype(jnp.bfloat16)


def mm_split(a, b):
    (a_high, a_low), (b_high, b_low) = a, b
    return mm(jnp.concatenate([a_high, a_high, a_low], axis=1), jnp.concatenate([b_high, b_low, b_high], axis=0))


def split3(x):
    high = x.astype(jnp.bfloat16).astype(jnp.float32)
    rest = x - high
    mid = rest.astype(jnp.bfloat16).astype(jnp.float32)
    return high, mid, rest - mid


def pack_kernel(rows_ref, points_ref, vectors_ref, leaf_ref, node_ref, out_ref, stage):
    width = vectors_ref.shape[0]
    half = LANES // 2
    low = iota((1, LANES), 1) < half
    stage[...] = jnp.zeros_like(stage)
    stage[0:1, 0:half] = leaf_ref[...].astype(jnp.float32)
    stage[1:5, 0:half] = node_ref[0].astype(jnp.float32)
    stage[5:8, 0:width] = points_ref[...].astype(jnp.float32)
    s = stage[...]
    index = s[0:1]
    index = (index + swap_halves(jnp.broadcast_to(index, (SUB, LANES)))[0:1]).astype(jnp.int32)
    index = jnp.broadcast_to(index, (SUB, LANES))
    stage[0:3, :] = rows_ref[:, 0:LANES]
    found = jnp.zeros((SUB, LANES), jnp.float32)
    for tile in range(rows_ref.shape[1] // LANES):
        stage[0:3, :] = rows_ref[:, tile * LANES : (tile + 1) * LANES]
        picked = take_lanes(stage[...], index & (LANES - 1))
        found = jnp.where(index // LANES == tile, picked, found)
    high, mid, tail = split3(found)
    swapped = swap_halves(s)
    lines = [
        jnp.where(low, high[0:1], mid[0:1]),
        jnp.where(low, tail[0:1], high[1:2]),
        jnp.where(low, mid[1:2], tail[1:2]),
        jnp.where(low, high[2:3], mid[2:3]),
        tail[2:3],
        jnp.where(low, s[1:2], swapped[2:3]),
        jnp.where(low, s[3:4], swapped[4:5]),
        s[5:6] + pltpu.roll(s, width, axis=1)[6:7] + pltpu.roll(s, 2 * width, axis=1)[7:8],
    ]
    block = jnp.concatenate([vectors_ref[...].astype(jnp.float32)] + lines, axis=0).astype(jnp.bfloat16)

    def put(device, unused):
        out_ref[device] = block
        return unused

    lax.fori_loop(0, out_ref.shape[0], put, 0)


def evaluate(dist):
    inverse = lax.rsqrt(dist)
    turns = dist * inverse
    f = turns - jnp.round(turns)
    u = f * f
    scale = math.sqrt(TURNS)
    sine = SIN_POLY[-1] * scale
    cosine = COS_POLY[-1] * scale
    for value in SIN_POLY[-2::-1]:
        sine = sine * u + value * scale
    for value in COS_POLY[-2::-1]:
        cosine = cosine * u + value * scale
    sine = sine * f
    real = (TURNS - sine * sine) * inverse
    imag = (sine * cosine) * inverse
    return real.astype(jnp.bfloat16), imag.astype(jnp.bfloat16)


def main_kernel(levels, got_ref, rows_ref, interp_ref, maps_ref, top_ref, left_ref, kre_ref, kim_ref, samples_ref):
    half = LANES // 2
    leaf = lax.axis_index("rows")
    column = lax.axis_index("cols")
    cols = lax.axis_size("cols")
    group_leaves = 2**levels
    group_devices = group_leaves * cols
    devices = got_ref.shape[0]
    width = got_ref.shape[1] - SUB
    width_bits = width.bit_length() - 1
    lane8 = iota((SUB, LANES), 1)
    sub8 = iota((SUB, LANES), 0)
    low8 = lane8 < half
    member = leaf & (group_leaves - 1)
    mine = sub8 == member >> 1

    group_start = (leaf // group_leaves) * group_devices
    extra = got_ref[pl.ds(group_start, group_devices), width : width + SUB, :].astype(jnp.float32)
    extra = extra.reshape(group_devices * SUB, LANES).astype(jnp.bfloat16)
    shape = (7 * 16, group_devices * SUB)
    at = iota(shape, 0)
    source = ((at & 7) * 2 + ((at >> 3) & 1)) * (cols * SUB) + (at >> 4)
    picked = mm((iota(shape, 1) == source).astype(jnp.bfloat16), extra)
    even = [picked[r * 16 : r * 16 + 8] for r in range(7)]
    odd = [picked[r * 16 + 8 : r * 16 + 16] for r in range(7)]
    even_s = [swap_halves(v) for v in even]
    odd_s = [swap_halves(v) for v in odd]
    coords = [
        jnp.where(low8, even[0] + even_s[0] + even[1], odd[0] + odd_s[0] + odd_s[1]),
        jnp.where(low8, even_s[1] + (even[2] + even_s[2]), odd[1] + (odd[2] + odd_s[2])),
        jnp.where(low8, even[3] + even_s[3] + even[4], odd[3] + odd_s[3] + odd[4]),
    ]
    lists = [
        jnp.where(low8, even[5], even_s[5]).astype(jnp.int32),
        jnp.where(low8, even_s[5], even[5]).astype(jnp.int32),
        jnp.where(low8, even[6], even_s[6]).astype(jnp.int32),
        jnp.where(low8, even_s[6], even[6]).astype(jnp.int32),
    ]

    def own_row(x):
        return jnp.sum(jnp.where(mine, x, jnp.zeros_like(x)), axis=0, keepdims=True)

    siblings = []
    own_lists = [own_row(lists[0])]
    stacked = coords
    for level in range(1, levels):
        own = [take_lanes(v, lists[level - 1]) for v in stacked]
        step = 2 ** (level - 1)
        upper = (sub8 & step) != 0
        other = [jnp.where(upper, pltpu.roll(v, step, axis=0), pltpu.roll(v, SUB - step, axis=0)) for v in own]
        siblings.append([own_row(v) for v in other])
        stacked = [jnp.where(low8 == upper, b, a) for a, b in zip(own, other)]
        own_lists.append(own_row(lists[level]))
    low1 = iota((1, LANES), 1) < half
    tiles = [[own_row(v) for v in coords]]
    tiles.append([jnp.where(low1, a, b) for a, b in zip(siblings[0], siblings[1])])
    tiles.append(siblings[2])
    tree_lanes = len(tiles) * LANES
    own_rows = rows_ref.shape[1] // cols
    start = pl.multiple_of(column * own_rows, LANES)
    own_points = rows_ref[:, pl.ds(start, own_rows)]

    def right_side(points):
        lanes = points[0].shape[1]
        lines = []
        norm = jnp.full((1, lanes), SMOOTH * SMOOTH, jnp.float32)
        for x in points:
            norm = norm + x * x
            lines += split3(x * (-2 * TURNS * TURNS))
        for repeat in range(6):
            lines += [jnp.full((1, lanes), v, jnp.float32) for v in SCALE_PARTS]
        lines += split3(norm * (TURNS * TURNS))
        lines.append(jnp.zeros((LANES - len(lines), lanes), jnp.float32))
        return jnp.concatenate(lines, axis=0).astype(jnp.bfloat16)

    right_tree = jnp.concatenate([right_side(t) for t in tiles], axis=1)
    right_own = right_side([own_points[c : c + 1] for c in range(3)])

    block_devices = min(devices, group_devices)
    single = block_devices == devices
    block = block_devices * width
    vec_count = got_ref.shape[2]
    eye = (iota((vec_count, vec_count), 0) == iota((vec_count, vec_count), 1)).astype(jnp.bfloat16)
    shape = (block, block_devices * SUB)
    spread = (iota(shape, 1) == ((iota(shape, 0) >> width_bits) * SUB + SUB - 1)).astype(jnp.bfloat16)
    shape = (block, LANES)
    lane_of = iota(shape, 1)
    keep = (((lane_of ^ iota(shape, 0)) & (width - 1)) == 0) & (lane_of < 3 * width)
    ones = ((lane_of >= 27) & (lane_of < 30)).astype(jnp.bfloat16)
    shape = (LANES, LANES)
    away = iota(shape, 1) - 3 * (iota(shape, 0) >> width_bits)
    within = iota(shape, 0) < 3 * width
    collect = jnp.concatenate(
        [(within & (away >= first) & (away < first + 3)).astype(jnp.bfloat16) for first in (0, 9, 18)], axis=0
    )

    def panel_vectors(number):
        got = got_ref[pl.ds(number * block_devices, block_devices), 0:width, :].astype(jnp.float32)
        vectors = got.reshape(block, vec_count).astype(jnp.bfloat16)
        return mm(eye, vectors, dims=((1,), (1,))).astype(jnp.bfloat16)

    def panel_left(number):
        tail = got_ref[pl.ds(number * block_devices, block_devices), width : width + SUB, :].astype(jnp.float32)
        tail = tail.reshape(block_devices * SUB, LANES).astype(jnp.bfloat16)
        points = jnp.where(keep, mm(spread, tail), 0.0)
        high, low = split2(points * points)
        left_ref[...] = mm(jnp.concatenate([points.astype(jnp.bfloat16), high, low], axis=1), collect).astype(jnp.bfloat16) + ones

    def fill(at, count, right, lane):
        dist = mm(left_ref[pl.ds(at, count), :], right)
        lanes = right.shape[1]
        kre_ref[pl.ds(at, count), lane : lane + lanes], kim_ref[pl.ds(at, count), lane : lane + lanes] = evaluate(dist)

    def sample(vectors, lane, lanes):
        both = [mm(vectors, k[:, lane : lane + lanes]) for k in (kre_ref, kim_ref)]
        return jnp.concatenate(both, axis=0)

    chunk = min(LANES, block)
    panel_left(0)
    vectors = panel_vectors(0)
    for at in range(0, block, chunk):
        fill(at, chunk, right_tree, 0)
    samples_ref[:, 0:tree_lanes] = sample(vectors, 0, tree_lanes)
    if not single:
        for at in range(0, block, chunk):
            fill(at, chunk, right_own, tree_lanes)
        samples_ref[:, tree_lanes:] = sample(vectors, tree_lanes, own_rows)

        def more(number, unused):
            panel_left(number)
            for at in range(0, block, chunk):
                fill(at, chunk, right_tree, 0)
                fill(at, chunk, right_own, tree_lanes)
            samples_ref[...] += sample(panel_vectors(number), 0, tree_lanes + own_rows)
            return unused

        lax.fori_loop(1, devices // block_devices, more, 0)

    full = (2 * vec_count, LANES)
    low = iota(full, 1) < half
    pair0 = samples_ref[:, 0:LANES]
    pair0_s = swap_halves(pair0)
    pair12 = samples_ref[:, LANES : 2 * LANES]
    pair12_s = swap_halves(pair12)
    pair3 = samples_ref[:, 2 * LANES : 3 * LANES]

    def is_upper(level, shape):
        return (jnp.full(shape, member, jnp.int32) & 2**level) != 0

    upper0 = is_upper(0, full)
    stacks = [pair0]
    skels = [jnp.where(upper0 == low, pair0_s, pair0)]
    for level in range(levels):
        picked = take_lanes(stacks[level], jnp.broadcast_to(own_lists[level], full))
        skels.append(picked)
        if level + 1 < levels:
            up = is_upper(level + 1, full)
            if level == 0:
                other = jnp.where(up, pair12, pair12_s)
            elif level == 1:
                other = jnp.where(up, pair12_s, pair12)
            else:
                other = pair3
            stacks.append(jnp.where(low == up, other, picked))

    two = [jnp.where(low, skels[0], skels[1]).T, jnp.where(low, skels[2], skels[3]).T, skels[4].T]
    row_form = [two[0][0:half], two[0][half:], two[1][0:half], two[1][half:], two[2][0:half]]
    top_ref[0] = row_form[4]
    row_form = [split2(v) for v in row_form]

    stacks = [split2(v) for v in stacks]
    square = (half, LANES)
    low64 = iota(square, 1) < half
    right_maps = [mm_split(row_form[level + 1], stacks[level]) for level in range(levels)]
    gram = mm_split(row_form[0], stacks[0])
    grams = [jnp.where(is_upper(0, square) == low64, swap_halves(gram), gram)]
    for level in range(levels):
        grams.append(take_lanes(right_maps[level], jnp.broadcast_to(own_lists[level], square)))
    pairs = []
    diagonal = iota(square, 0) == (iota(square, 1) & (half - 1))
    for a, b in ((0, 1), (2, 3), (4, 4)):
        gram = jnp.where(low64, grams[a], grams[b])
        trace = jnp.sum(jnp.where(diagonal, gram, 0.0), axis=0, keepdims=True)
        first = jnp.sum(jnp.where(low1, trace, 0.0), axis=1, keepdims=True)
        second = jnp.sum(jnp.where(low1, 0.0, trace), axis=1, keepdims=True)
        trace = jnp.where(low1, first, second)
        ridge = RIDGE * (2 * vec_count) * (trace * (1.0 / (half * 2 * vec_count)) + EPSILON)
        gram = gram + jnp.where(diagonal, ridge, 0.0)
        pairs.append([gram[r * SUB : (r + 1) * SUB] for r in range(half // SUB)])

    where_in_half = lane8 & (half - 1)
    half_base = lane8 - where_in_half
    blocks = half // SUB
    piece = block // blocks

    def spread_row(x, row):
        return jnp.broadcast_to(x[row : row + 1], (SUB, LANES))

    zero8 = jnp.zeros((SUB, LANES), jnp.float32)
    for turn in range(blocks):
        first = turn * SUB
        ahead = turn + 1 if turn + 1 < blocks else None
        within_turn = (where_in_half >> 3) == turn
        diagonals = [[take_lanes(a[turn], half_base + (first + j)) for j in range(SUB)] for a in pairs]
        if ahead is not None:
            nexts = [[take_lanes(a[ahead], half_base + (first + j)) for j in range(SUB)] for a in pairs]
        lines = [a[turn] for a in pairs]
        for s in range(SUB):
            if single and s % 2 == 0:
                fill(turn * piece + s // 2 * (piece // 4), piece // 4, right_own, tree_lanes)
            here = where_in_half == first + s
            row = sub8 == s
            for n in range(len(pairs)):
                columns = diagonals[n]
                inverse = 1.0 / spread_row(columns[s], s)
                column = jnp.where(row, -1.0, columns[s])
                line = jnp.where(here, 1.0, spread_row(lines[n], s)) * inverse
                lines[n] = jnp.where(here | row, 0.0, lines[n]) - column * line
                for j in range(s + 1, SUB):
                    factor = spread_row(columns[j], s) * inverse
                    columns[j] = jnp.where(row, 0.0, columns[j]) - column * factor
        for n, a in enumerate(pairs):
            line = lines[n]
            cleared = [jnp.where(within_turn, 0.0, v) for v in a]
            others = [b for b in range(blocks) if b not in (turn, ahead)]
            if ahead is not None:
                terms = [nexts[n][j] * spread_row(line, j) for j in range(SUB)]
                while len(terms) > 1:
                    terms = [x + y for x, y in zip(terms[::2], terms[1::2])]
            stacked = [zero8] * (2 * blocks)
            stacked[turn] = jnp.where(low8, line, 0.0)
            stacked[blocks + turn] = jnp.where(low8, 0.0, line)
            left = split2(jnp.concatenate([a[b] for b in others], axis=0))
            product = mm_split(left, split2(jnp.concatenate(stacked, axis=0)))
            for number, b in enumerate(others):
                a[b] = cleared[b] - product[number * SUB : (number + 1) * SUB]
            if ahead is not None:
                a[ahead] = cleared[ahead] - terms[0]
            a[turn] = line

    inverses = []
    for a in pairs:
        both = jnp.concatenate(a, axis=0)
        inverses.append(split2(jnp.concatenate([jnp.where(low64, both, 0.0), jnp.where(low64, 0.0, both)], axis=0)))
    if single:
        own_samples = sample(vectors, tree_lanes, own_rows)
    else:
        own_samples = samples_ref[:, tree_lanes:]
    right_leaf = mm_split(row_form[0], split2(own_samples))

    def rows_from(pair, first, last):
        return pair[0][first:last], pair[1][first:last]

    result = mm_split(inverses[1], split2(jnp.concatenate([right_maps[1], right_maps[2]], axis=0)))
    maps_ref[0, 1] = result[0:half]
    maps_ref[0, 2] = result[half:]
    zero = jnp.zeros((half, LANES), jnp.float32)
    maps_ref[0, 3] = mm_split(rows_from(inverses[2], 0, half), split2(jnp.concatenate([right_maps[3], zero], axis=0)))
    maps_ref[0, 0] = mm_split(rows_from(inverses[0], half, LANES), split2(jnp.concatenate([zero, right_maps[0]], axis=0)))
    zero = jnp.zeros((half, own_rows), jnp.float32)
    interp_ref[...] = mm_split(rows_from(inverses[0], 0, half), split2(jnp.concatenate([right_leaf, zero], axis=0)))


def body(row_points, panel_points, test_vectors, leaf_skeleton, node_skeleton):
    devices = lax.axis_size("rows") * lax.axis_size("cols")
    vec_count, width = test_vectors.shape
    rows_here = row_points.shape[1]
    levels, skel = node_skeleton.shape[1:]
    packed = pl.pallas_call(
        pack_kernel,
        out_shape=jax.ShapeDtypeStruct((devices, width + SUB, vec_count), jnp.bfloat16),
        in_specs=[VMEM] * 5,
        out_specs=VMEM,
        scratch_shapes=[pltpu.VMEM((SUB, LANES), jnp.float32)],
    )(row_points, panel_points, test_vectors.T, leaf_skeleton, node_skeleton)
    got = lax.all_to_all(packed, ("rows", "cols"), 0, 0, tiled=True)
    own_rows = rows_here // lax.axis_size("cols")
    lanes = 3 * LANES + own_rows
    block = min(devices, 2**levels * lax.axis_size("cols")) * width
    return pl.pallas_call(
        functools.partial(main_kernel, levels),
        out_shape=(
            jax.ShapeDtypeStruct((skel, own_rows), jnp.float32),
            jax.ShapeDtypeStruct((1, levels, skel, 2 * skel), jnp.float32),
            jax.ShapeDtypeStruct((1, skel, 2 * vec_count), jnp.float32),
        ),
        in_specs=[VMEM] * 2,
        out_specs=(VMEM, VMEM, VMEM),
        scratch_shapes=[
            pltpu.VMEM((block, LANES), jnp.bfloat16),
            pltpu.VMEM((block, lanes), jnp.bfloat16),
            pltpu.VMEM((block, lanes), jnp.bfloat16),
            pltpu.VMEM((2 * vec_count, lanes), jnp.float32),
        ],
    )(got, row_points)


def solution(mesh):
    placed = (
        P(None, "rows"),
        P(None, ("rows", "cols")),
        P(None, ("rows", "cols")),
        P("rows", None),
        P("rows", None, None),
    )
    return jax.shard_map(
        body,
        mesh=mesh,
        in_specs=placed,
        out_specs=(P(None, ("rows", "cols")), P("rows", None, None, None), P("rows", None, None)),
        check_vma=False,
    )
```

time: 31.3 us -> 25.6 us (0.82)
  Pallas kernels: 12.5 us -> 8.36 us
  local copies, waits for them, and re-layouts: 1.4 us -> 0 us
    pallas_call x1, Pallas kernels: 10.7 us -> 6.6 us  [body(): pl.pallas_call(functools.partial(main_kernel, levels), out_shape=(jax.Sha...]
    unnamed x1 -> x0, local copies, waits for them, and re-layouts: 1.4 us -> none
where the time goes in v2:
time: 25.6 us; the launch traced here: 25.4 us
  blocking collectives  16.4 us (64%)
  Pallas kernels  8.36 us (33%)
  between operations  0.63 us (2%)
    all_to_all x1, blocking collectives, body(): got = lax.all_to_all(packed, ('rows', 'cols'), 0, 0, tiled=True)  16.4 us
    pallas_call x1, Pallas kernels, body(): pl.pallas_call(functools.partial(main_kernel, levels), out_shape=(jax.Sha...  6.6 us
    pallas_call x1, Pallas kernels, body(): pl.pallas_call(pack_kernel, out_shape=jax.ShapeDtypeStruct((devices, widt...  1.76 us

profile of v2, /device:TPU:1, one launch (start us, length us, event | category | flops | bytes accessed | tf_op | source)
XLA Modules:
  0.0 25.4 jit_solution(5583548965067421339)
XLA Ops:
  0.6 1.8 %shard_map.76 = bf16[32,24,128]{2,1,0:T(8,128)(2,1)} custom-call(f32[3,512]{1,0:T(4,128)} %rows_ref.3, bf16[3,16]{1,0:T(4,128)(2,1)} %points_ref.1, bf16[16,128]{1,0:T(8,128)(2,1)} %bitcast.1, s32[1,64]{1,0:T(1,128)} %leaf_ref.1, s32[1,4,64]{2,1,0:T(4,128)} %node_ref.1), custom_call_target="tpu_custom_call" | custom-call | tf_op jit(solution)/shard_map/pallas_call | solution.py:395
  2.4 16.4 %all_to_all.5.got_ref = bf16[32,24,128]{2,1,0:T(8,128)(2,1)} all-to-all(bf16[32,24,128]{2,1,0:T(8,128)(2,1)} %shard_map.76), channel_id=1, replica_groups=mesh['rows'=16,'cols'=2] {'rows','cols'}, dimensions={0} | all-to-all | bytes 393216 | tf_op jit(solution)/shard_map/all_to_all | solution.py:402
  18.8 6.6 %shard_map.77 = (f32[64,256]{1,0:T(8,128)}, f32[1,4,64,128]{3,2,1,0:T(8,128)}, f32[1,64,256]{2,1,0:T(8,128)}) custom-call(bf16[32,24,128]{2,1,0:T(8,128)(2,1)} %all_to_all.5.got_ref, f32[3,512]{1,0:T(4,128)} %rows_ref.3), custom_call_target="tpu_custom_call" | custom-call | tf_op jit(solution)/shard_map/pallas_call | solution.py:406

commit v3 on v2

--- a/solution.py
+++ b/solution.py
@@ -394,7 +394,7 @@
     levels, skel = node_skeleton.shape[1:]
     packed = pl.pallas_call(
         pack_kernel,
-        out_shape=jax.ShapeDtypeStruct((devices, width + SUB, vec_count), jnp.bfloat16),
+        out_shape=pltpu.VMEM((devices, width + SUB, vec_count), jnp.bfloat16),
         in_specs=[VMEM] * 5,
         out_specs=VMEM,
         scratch_shapes=[pltpu.VMEM((SUB, LANES), jnp.float32)],
@@ -418,7 +418,7 @@
             pltpu.VMEM((block, lanes), jnp.bfloat16),
             pltpu.VMEM((2 * vec_count, lanes), jnp.float32),
         ],
-    )(got, row_points)
+    )(pltpu.with_memory_space_constraint(got, pltpu.VMEM), row_points)
 
 
 def solution(mesh):

time: 25.6 us -> 24.4 us (0.953)
  Pallas kernels: 8.36 us -> 7.46 us
  blocking collectives: 16.4 us -> 16.1 us
    pallas_call x1, Pallas kernels: 1.76 us -> 1.08 us  [body(): pl.pallas_call(pack_kernel, out_shape=pltpu.VMEM((devices, width + SUB, v...]
    all_to_all x1, blocking collectives: 16.4 us -> 16.1 us  [body(): got = lax.all_to_all(packed, ('rows', 'cols'), 0, 0, tiled=True)]
where the time goes in v3:
time: 24.4 us; the launch traced here: 24.2 us
  blocking collectives  16.1 us (66%)
  Pallas kernels  7.46 us (31%)
  between operations  0.64 us (3%)
    all_to_all x1, blocking collectives, body(): got = lax.all_to_all(packed, ('rows', 'cols'), 0, 0, tiled=True)  16.1 us
    pallas_call x1, Pallas kernels, body(): pl.pallas_call(functools.partial(main_kernel, levels), out_shape=(jax.Sha...  6.38 us
    pallas_call x1, Pallas kernels, body(): pl.pallas_call(pack_kernel, out_shape=pltpu.VMEM((devices, width + SUB, v...  1.08 us

profile of v3, /device:TPU:1, one launch (start us, length us, event | category | flops | bytes accessed | tf_op | source)
XLA Modules:
  0.0 24.2 jit_solution(10428616865327346555)
XLA Ops:
  0.6 1.1 %shard_map.76 = bf16[32,24,128]{2,1,0:T(8,128)(2,1)S(1)} custom-call(f32[3,512]{1,0:T(4,128)} %rows_ref.3, bf16[3,16]{1,0:T(4,128)(2,1)} %points_ref.1, bf16[16,128]{1,0:T(8,128)(2,1)} %bitcast.1, s32[1,64]{1,0:T(1,128)} %leaf_ref.1, s32[1,4,64]{2,1,0:T(4,128)} %node_ref.1), custom_call_target="tpu_custom_call" | custom-call | tf_op jit(solution)/shard_map/pallas_call | solution.py:395
  1.7 16.1 %all_to_all.5.got_ref = bf16[32,24,128]{2,1,0:T(8,128)(2,1)S(1)} all-to-all(bf16[32,24,128]{2,1,0:T(8,128)(2,1)S(1)} %shard_map.76), channel_id=1, replica_groups=mesh['rows'=16,'cols'=2] {'rows','cols'}, dimensions={0} | all-to-all | bytes 393216 | tf_op jit(solution)/shard_map/all_to_all | solution.py:402
  17.8 6.4 %shard_map.77 = (f32[64,256]{1,0:T(8,128)}, f32[1,4,64,128]{3,2,1,0:T(8,128)}, f32[1,64,256]{2,1,0:T(8,128)}) custom-call(bf16[32,24,128]{2,1,0:T(8,128)(2,1)S(1)} %all_to_all.5.got_ref, f32[3,512]{1,0:T(4,128)} %rows_ref.3), custom_call_target="tpu_custom_call" | custom-call | tf_op jit(solution)/shard_map/pallas_call | solution.py:406

commit v4 on v3

--- a/solution.py
+++ b/solution.py
@@ -67,7 +67,8 @@
     return high, mid, rest - mid
 
 
-def pack_kernel(rows_ref, points_ref, vectors_ref, leaf_ref, node_ref, out_ref, stage):
+def pack_kernel(rows_ref, points_ref, vectors_ref, leaf_ref, node_ref, out_ref, kept_ref, stage):
+    kept_ref[...] = rows_ref[...]
     width = vectors_ref.shape[0]
     half = LANES // 2
     low = iota((1, LANES), 1) < half
@@ -106,6 +107,12 @@
     lax.fori_loop(0, out_ref.shape[0], put, 0)
 
 
+SETUP_PIECES = 4
+STAGE_PIECES = 4
+TURN_PIECES = (0, 0, 0, 0, 0, 0, 0, 0)
+LEAF_TURN = 3
+
+
 def evaluate(dist):
     inverse = lax.rsqrt(dist)
     turns = dist * inverse
@@ -140,6 +147,72 @@
     member = leaf & (group_leaves - 1)
     mine = sub8 == member >> 1
 
+    tree_lanes = 3 * LANES
+    own_rows = rows_ref.shape[1] // cols
+    start = pl.multiple_of(column * own_rows, LANES)
+    own_points = rows_ref[:, pl.ds(start, own_rows)]
+
+    def right_side(points):
+        lanes = points[0].shape[1]
+        lines = []
+        norm = jnp.full((1, lanes), SMOOTH * SMOOTH, jnp.float32)
+        for x in points:
+            norm = norm + x * x
+            lines += split3(x * (-2 * TURNS * TURNS))
+        for repeat in range(6):
+            lines += [jnp.full((1, lanes), v, jnp.float32) for v in SCALE_PARTS]
+        lines += split3(norm * (TURNS * TURNS))
+        lines.append(jnp.zeros((LANES - len(lines), lanes), jnp.float32))
+        return jnp.concatenate(lines, axis=0).astype(jnp.bfloat16)
+
+    block_devices = min(devices, group_devices)
+    single = block_devices == devices
+    block = block_devices * width
+    vec_count = got_ref.shape[2]
+    eye = (iota((vec_count, vec_count), 0) == iota((vec_count, vec_count), 1)).astype(jnp.bfloat16)
+    shape = (width, LANES)
+    lane_of = iota(shape, 1)
+    keep = (((lane_of ^ iota(shape, 0)) & (width - 1)) == 0) & (lane_of < 3 * width)
+    ones = ((iota((1, LANES), 1) >= 27) & (iota((1, LANES), 1) < 30)).astype(jnp.float32)
+    shape = (LANES, LANES)
+    away = iota(shape, 1) - 3 * (iota(shape, 0) >> width_bits)
+    within = iota(shape, 0) < 3 * width
+    collect = jnp.concatenate(
+        [(within & (away >= first) & (away < first + 3)).astype(jnp.bfloat16) for first in (0, 9, 18)], axis=0
+    )
+
+    def panel_vectors(number):
+        got = got_ref[pl.ds(number * block_devices, block_devices), 0:width, :].astype(jnp.float32)
+        vectors = got.reshape(block, vec_count).astype(jnp.bfloat16)
+        return mm(eye, vectors, dims=((1,), (1,))).astype(jnp.bfloat16)
+
+    def panel_left(number):
+        tail = got_ref[pl.ds(number * block_devices, block_devices), width : width + SUB, :].astype(jnp.float32)
+        points = [jnp.where(keep, jnp.broadcast_to(tail[d, SUB - 1 : SUB], keep.shape), 0.0) for d in range(block_devices)]
+        points = jnp.concatenate(points, axis=0)
+        high, low = split2(points * points)
+        left = mm(jnp.concatenate([points.astype(jnp.bfloat16), high, low], axis=1), collect) + ones
+        left_ref[...] = left.astype(jnp.bfloat16)
+
+    def fill(at, count, right, lane):
+        dist = mm(left_ref[pl.ds(at, count), :], right)
+        lanes = right.shape[1]
+        kre_ref[pl.ds(at, count), lane : lane + lanes], kim_ref[pl.ds(at, count), lane : lane + lanes] = evaluate(dist)
+
+    def sample(vectors, lane, lanes):
+        both = [mm(vectors, k[:, lane : lane + lanes]) for k in (kre_ref, kim_ref)]
+        return jnp.concatenate(both, axis=0)
+
+    chunk = min(LANES, block)
+    panel_left(0)
+    right_own = right_side([own_points[c : c + 1] for c in range(3)])
+    pieces = list(range(0, block, 16)) if single else []
+
+    def own_pieces(count):
+        for unused in range(min(count, len(pieces))):
+            fill(pieces.pop(0), 16, right_own, tree_lanes)
+
+    vectors = panel_vectors(0)
     group_start = (leaf // group_leaves) * group_devices
     extra = got_ref[pl.ds(group_start, group_devices), width : width + SUB, :].astype(jnp.float32)
     extra = extra.reshape(group_devices * SUB, LANES).astype(jnp.bfloat16)
@@ -177,73 +250,13 @@
         siblings.append([own_row(v) for v in other])
         stacked = [jnp.where(low8 == upper, b, a) for a, b in zip(own, other)]
         own_lists.append(own_row(lists[level]))
+        own_pieces(SETUP_PIECES)
     low1 = iota((1, LANES), 1) < half
     tiles = [[own_row(v) for v in coords]]
     tiles.append([jnp.where(low1, a, b) for a, b in zip(siblings[0], siblings[1])])
     tiles.append(siblings[2])
-    tree_lanes = len(tiles) * LANES
-    own_rows = rows_ref.shape[1] // cols
-    start = pl.multiple_of(column * own_rows, LANES)
-    own_points = rows_ref[:, pl.ds(start, own_rows)]
-
-    def right_side(points):
-        lanes = points[0].shape[1]
-        lines = []
-        norm = jnp.full((1, lanes), SMOOTH * SMOOTH, jnp.float32)
-        for x in points:
-            norm = norm + x * x
-            lines += split3(x * (-2 * TURNS * TURNS))
-        for repeat in range(6):
-            lines += [jnp.full((1, lanes), v, jnp.float32) for v in SCALE_PARTS]
-        lines += split3(norm * (TURNS * TURNS))
-        lines.append(jnp.zeros((LANES - len(lines), lanes), jnp.float32))
-        return jnp.concatenate(lines, axis=0).astype(jnp.bfloat16)
-
     right_tree = jnp.concatenate([right_side(t) for t in tiles], axis=1)
-    right_own = right_side([own_points[c : c + 1] for c in range(3)])
-
-    block_devices = min(devices, group_devices)
-    single = block_devices == devices
-    block = block_devices * width
-    vec_count = got_ref.shape[2]
-    eye = (iota((vec_count, vec_count), 0) == iota((vec_count, vec_count), 1)).astype(jnp.bfloat16)
-    shape = (block, block_devices * SUB)
-    spread = (iota(shape, 1) == ((iota(shape, 0) >> width_bits) * SUB + SUB - 1)).astype(jnp.bfloat16)
-    shape = (block, LANES)
-    lane_of = iota(shape, 1)
-    keep = (((lane_of ^ iota(shape, 0)) & (width - 1)) == 0) & (lane_of < 3 * width)
-    ones = ((lane_of >= 27) & (lane_of < 30)).astype(jnp.bfloat16)
-    shape = (LANES, LANES)
-    away = iota(shape, 1) - 3 * (iota(shape, 0) >> width_bits)
-    within = iota(shape, 0) < 3 * width
-    collect = jnp.concatenate(
-        [(within & (away >= first) & (away < first + 3)).astype(jnp.bfloat16) for first in (0, 9, 18)], axis=0
-    )
-
-    def panel_vectors(number):
-        got = got_ref[pl.ds(number * block_devices, block_devices), 0:width, :].astype(jnp.float32)
-        vectors = got.reshape(block, vec_count).astype(jnp.bfloat16)
-        return mm(eye, vectors, dims=((1,), (1,))).astype(jnp.bfloat16)
-
-    def panel_left(number):
-        tail = got_ref[pl.ds(number * block_devices, block_devices), width : width + SUB, :].astype(jnp.float32)
-        tail = tail.reshape(block_devices * SUB, LANES).astype(jnp.bfloat16)
-        points = jnp.where(keep, mm(spread, tail), 0.0)
-        high, low = split2(points * points)
-        left_ref[...] = mm(jnp.concatenate([points.astype(jnp.bfloat16), high, low], axis=1), collect).astype(jnp.bfloat16) + ones
-
-    def fill(at, count, right, lane):
-        dist = mm(left_ref[pl.ds(at, count), :], right)
-        lanes = right.shape[1]
-        kre_ref[pl.ds(at, count), lane : lane + lanes], kim_ref[pl.ds(at, count), lane : lane + lanes] = evaluate(dist)
-
-    def sample(vectors, lane, lanes):
-        both = [mm(vectors, k[:, lane : lane + lanes]) for k in (kre_ref, kim_ref)]
-        return jnp.concatenate(both, axis=0)
-
-    chunk = min(LANES, block)
-    panel_left(0)
-    vectors = panel_vectors(0)
+
     for at in range(0, block, chunk):
         fill(at, chunk, right_tree, 0)
     samples_ref[:, 0:tree_lanes] = sample(vectors, 0, tree_lanes)
@@ -279,6 +292,7 @@
     for level in range(levels):
         picked = take_lanes(stacks[level], jnp.broadcast_to(own_lists[level], full))
         skels.append(picked)
+        own_pieces(STAGE_PIECES)
         if level + 1 < levels:
             up = is_upper(level + 1, full)
             if level == 0:
@@ -314,15 +328,21 @@
         gram = gram + jnp.where(diagonal, ridge, 0.0)
         pairs.append([gram[r * SUB : (r + 1) * SUB] for r in range(half // SUB)])
 
+    right_maps = [split2(v) for v in right_maps]
     where_in_half = lane8 & (half - 1)
     half_base = lane8 - where_in_half
     blocks = half // SUB
-    piece = block // blocks
 
     def spread_row(x, row):
         return jnp.broadcast_to(x[row : row + 1], (SUB, LANES))
 
+    def total_of(terms):
+        while len(terms) > 1:
+            terms = [x + y for x, y in zip(terms[::2], terms[1::2])]
+        return terms[0]
+
     zero8 = jnp.zeros((SUB, LANES), jnp.float32)
+    zero16 = jnp.zeros((2 * SUB, LANES), jnp.bfloat16)
     for turn in range(blocks):
         first = turn * SUB
         ahead = turn + 1 if turn + 1 < blocks else None
@@ -332,59 +352,63 @@
             nexts = [[take_lanes(a[ahead], half_base + (first + j)) for j in range(SUB)] for a in pairs]
         lines = [a[turn] for a in pairs]
         for s in range(SUB):
-            if single and s % 2 == 0:
-                fill(turn * piece + s // 2 * (piece // 4), piece // 4, right_own, tree_lanes)
+            own_pieces(TURN_PIECES[turn] if s % 2 == 0 else 0)
             here = where_in_half == first + s
             row = sub8 == s
+            pivots = [spread_row(columns[s], s) for columns in diagonals]
+            inverses = 1.0 / jnp.where(sub8 == 0, pivots[0], jnp.where(sub8 == 1, pivots[1], pivots[2]))
             for n in range(len(pairs)):
                 columns = diagonals[n]
-                inverse = 1.0 / spread_row(columns[s], s)
+                inverse = spread_row(inverses, n)
                 column = jnp.where(row, -1.0, columns[s])
                 line = jnp.where(here, 1.0, spread_row(lines[n], s)) * inverse
                 lines[n] = jnp.where(here | row, 0.0, lines[n]) - column * line
                 for j in range(s + 1, SUB):
                     factor = spread_row(columns[j], s) * inverse
                     columns[j] = jnp.where(row, 0.0, columns[j]) - column * factor
+        if turn == LEAF_TURN:
+            own_pieces(block)
+            own_samples = sample(vectors, tree_lanes, own_rows) if single else samples_ref[:, tree_lanes:]
+            right_leaf = split2(mm_split(row_form[0], split2(own_samples)))
         for n, a in enumerate(pairs):
             line = lines[n]
             cleared = [jnp.where(within_turn, 0.0, v) for v in a]
             others = [b for b in range(blocks) if b not in (turn, ahead)]
             if ahead is not None:
-                terms = [nexts[n][j] * spread_row(line, j) for j in range(SUB)]
-                while len(terms) > 1:
-                    terms = [x + y for x, y in zip(terms[::2], terms[1::2])]
-            stacked = [zero8] * (2 * blocks)
-            stacked[turn] = jnp.where(low8, line, 0.0)
-            stacked[blocks + turn] = jnp.where(low8, 0.0, line)
-            left = split2(jnp.concatenate([a[b] for b in others], axis=0))
-            product = mm_split(left, split2(jnp.concatenate(stacked, axis=0)))
+                a[ahead] = cleared[ahead] - total_of([nexts[n][j] * spread_row(line, j) for j in range(SUB)])
+
+            def placed(part):
+                pads = [zero16] * blocks
+                both = [part, zero8] if turn % 2 == 0 else [zero8, part]
+                for side, chosen in ((0, low8), (1, ~low8)):
+                    pads[side * blocks // 2 + turn // 2] = jnp.concatenate(
+                        [jnp.where(chosen, v, 0.0) for v in both], axis=0
+                    ).astype(jnp.bfloat16)
+                return jnp.concatenate(pads, axis=0)
+
+            high = line.astype(jnp.bfloat16).astype(jnp.float32)
+            right = placed(high), placed(line - high)
+            product = mm_split(split2(jnp.concatenate([a[b] for b in others], axis=0)), right)
             for number, b in enumerate(others):
                 a[b] = cleared[b] - product[number * SUB : (number + 1) * SUB]
-            if ahead is not None:
-                a[ahead] = cleared[ahead] - terms[0]
             a[turn] = line
 
     inverses = []
     for a in pairs:
         both = jnp.concatenate(a, axis=0)
         inverses.append(split2(jnp.concatenate([jnp.where(low64, both, 0.0), jnp.where(low64, 0.0, both)], axis=0)))
-    if single:
-        own_samples = sample(vectors, tree_lanes, own_rows)
-    else:
-        own_samples = samples_ref[:, tree_lanes:]
-    right_leaf = mm_split(row_form[0], split2(own_samples))
-
-    def rows_from(pair, first, last):
-        return pair[0][first:last], pair[1][first:last]
-
-    result = mm_split(inverses[1], split2(jnp.concatenate([right_maps[1], right_maps[2]], axis=0)))
+    def times(pair, first, last, parts):
+        left = [v[first:last] for v in pair]
+        return mm_split(left, [jnp.concatenate(p, axis=0) if len(p) > 1 else p[0] for p in zip(*parts)])
+
+    zero = [jnp.zeros((half, LANES), jnp.bfloat16)] * 2
+    wide = [jnp.zeros((half, own_rows), jnp.bfloat16)] * 2
+    result = times(inverses[1], 0, LANES, (right_maps[1], right_maps[2]))
     maps_ref[0, 1] = result[0:half]
     maps_ref[0, 2] = result[half:]
-    zero = jnp.zeros((half, LANES), jnp.float32)
-    maps_ref[0, 3] = mm_split(rows_from(inverses[2], 0, half), split2(jnp.concatenate([right_maps[3], zero], axis=0)))
-    maps_ref[0, 0] = mm_split(rows_from(inverses[0], half, LANES), split2(jnp.concatenate([zero, right_maps[0]], axis=0)))
-    zero = jnp.zeros((half, own_rows), jnp.float32)
-    interp_ref[...] = mm_split(rows_from(inverses[0], 0, half), split2(jnp.concatenate([right_leaf, zero], axis=0)))
+    maps_ref[0, 3] = times(inverses[2], 0, half, (right_maps[3], zero))
+    maps_ref[0, 0] = times(inverses[0], half, LANES, (zero, right_maps[0]))
+    interp_ref[...] = times(inverses[0], 0, half, (right_leaf, wide))
 
 
 def body(row_points, panel_points, test_vectors, leaf_skeleton, node_skeleton):
@@ -392,11 +416,14 @@
     vec_count, width = test_vectors.shape
     rows_here = row_points.shape[1]
     levels, skel = node_skeleton.shape[1:]
-    packed = pl.pallas_call(
+    packed, kept = pl.pallas_call(
         pack_kernel,
-        out_shape=pltpu.VMEM((devices, width + SUB, vec_count), jnp.bfloat16),
+        out_shape=(
+            pltpu.VMEM((devices, width + SUB, vec_count), jnp.bfloat16),
+            pltpu.VMEM(row_points.shape, jnp.float32),
+        ),
         in_specs=[VMEM] * 5,
-        out_specs=VMEM,
+        out_specs=(VMEM, VMEM),
         scratch_shapes=[pltpu.VMEM((SUB, LANES), jnp.float32)],
     )(row_points, panel_points, test_vectors.T, leaf_skeleton, node_skeleton)
     got = lax.all_to_all(packed, ("rows", "cols"), 0, 0, tiled=True)
@@ -418,7 +445,7 @@
             pltpu.VMEM((block, lanes), jnp.bfloat16),
             pltpu.VMEM((2 * vec_count, lanes), jnp.float32),
         ],
-    )(pltpu.with_memory_space_constraint(got, pltpu.VMEM), row_points)
+    )(pltpu.with_memory_space_constraint(got, pltpu.VMEM), pltpu.with_memory_space_constraint(kept, pltpu.VMEM))
 
 
 def solution(mesh):

time: 24.4 us -> 23.9 us (0.980)
  Pallas kernels: 7.46 us -> 6.94 us
    pallas_call x1, Pallas kernels: 6.38 us -> 5.86 us  [body(): pl.pallas_call(functools.partial(main_kernel, levels), out_shape=(jax.Sha...]
where the time goes in v4:
time: 23.9 us; the launch traced here: 23.7 us
  blocking collectives  16.1 us (67%)
  Pallas kernels  6.94 us (29%)
  between operations  0.64 us (3%)
    all_to_all x1, blocking collectives, body(): got = lax.all_to_all(packed, ('rows', 'cols'), 0, 0, tiled=True)  16.1 us
    pallas_call x1, Pallas kernels, body(): pl.pallas_call(functools.partial(main_kernel, levels), out_shape=(jax.Sha...  5.86 us
    pallas_call x1, Pallas kernels, body(): pl.pallas_call(pack_kernel, out_shape=(pltpu.VMEM((devices, width + SUB,...  1.08 us

profile of v4, /device:TPU:1, one launch (start us, length us, event | category | flops | bytes accessed | tf_op | source)
XLA Modules:
  0.0 23.7 jit_solution(4439659079610902645)
XLA Ops:
  0.6 1.1 %shard_map.76 = (bf16[32,24,128]{2,1,0:T(8,128)(2,1)S(1)}, f32[3,512]{1,0:T(4,128)S(1)}) custom-call(f32[3,512]{1,0:T(4,128)} %rows_ref.1, bf16[3,16]{1,0:T(4,128)(2,1)} %points_ref.1, bf16[16,128]{1,0:T(8,128)(2,1)} %bitcast.1, s32[1,64]{1,0:T(1,128)} %leaf_ref.1, s32[1,4,64]{2,1,0:T(4,128)} %node_ref.1), custom_call_target="tpu_custom_call" | custom-call | tf_op jit(solution)/shard_map/pallas_call | solution.py:419
  1.7 16.1 %all_to_all.5.got_ref = bf16[32,24,128]{2,1,0:T(8,128)(2,1)S(1)} all-to-all(bf16[32,24,128]{2,1,0:T(8,128)(2,1)S(1)} %get-tuple-element.5), channel_id=1, replica_groups=mesh['rows'=16,'cols'=2] {'rows','cols'}, dimensions={0} | all-to-all | bytes 393216 | tf_op jit(solution)/shard_map/all_to_all | solution.py:429
  17.8 5.9 %shard_map.77 = (f32[64,256]{1,0:T(8,128)}, f32[1,4,64,128]{3,2,1,0:T(8,128)}, f32[1,64,256]{2,1,0:T(8,128)}) custom-call(bf16[32,24,128]{2,1,0:T(8,128)(2,1)S(1)} %all_to_all.5.got_ref, f32[3,512]{1,0:T(4,128)S(1)} %get-tuple-element.6.rows_ref), custom_call_target="tpu_custom_call" | custom-call | tf_op jit(solution)/shard_map/pallas_call | solution.py:433

commit v5 on v4

--- a/solution.py
+++ b/solution.py
@@ -131,7 +131,7 @@
     return real.astype(jnp.bfloat16), imag.astype(jnp.bfloat16)
 
 
-def main_kernel(levels, got_ref, rows_ref, interp_ref, maps_ref, top_ref, left_ref, kre_ref, kim_ref, samples_ref):
+def main_kernel(levels, got_ref, rows_ref, interp_out, maps_out, top_out, interp_ref, maps_ref, top_ref, left_ref, kre_ref, kim_ref, samples_ref, sems):
     half = LANES // 2
     leaf = lax.axis_index("rows")
     column = lax.axis_index("cols")
@@ -306,6 +306,13 @@
     two = [jnp.where(low, skels[0], skels[1]).T, jnp.where(low, skels[2], skels[3]).T, skels[4].T]
     row_form = [two[0][0:half], two[0][half:], two[1][0:half], two[1][half:], two[2][0:half]]
     top_ref[0] = row_form[4]
+    copies = []
+
+    def send(source, target):
+        copies.append(pltpu.make_async_copy(source, target, sems.at[len(copies)]))
+        copies[-1].start()
+
+    send(top_ref, top_out)
     row_form = [split2(v) for v in row_form]
 
     stacks = [split2(v) for v in stacks]
@@ -317,6 +324,7 @@
     for level in range(levels):
         grams.append(take_lanes(right_maps[level], jnp.broadcast_to(own_lists[level], square)))
     pairs = []
+    scales = []
     diagonal = iota(square, 0) == (iota(square, 1) & (half - 1))
     for a, b in ((0, 1), (2, 3), (4, 4)):
         gram = jnp.where(low64, grams[a], grams[b])
@@ -325,7 +333,8 @@
         second = jnp.sum(jnp.where(low1, 0.0, trace), axis=1, keepdims=True)
         trace = jnp.where(low1, first, second)
         ridge = RIDGE * (2 * vec_count) * (trace * (1.0 / (half * 2 * vec_count)) + EPSILON)
-        gram = gram + jnp.where(diagonal, ridge, 0.0)
+        scales.append(RIDGE / ridge)
+        gram = gram * scales[-1] + jnp.where(diagonal, RIDGE, 0.0)
         pairs.append([gram[r * SUB : (r + 1) * SUB] for r in range(half // SUB)])
 
     right_maps = [split2(v) for v in right_maps]
@@ -354,18 +363,17 @@
         for s in range(SUB):
             own_pieces(TURN_PIECES[turn] if s % 2 == 0 else 0)
             here = where_in_half == first + s
-            row = sub8 == s
+            unit = jnp.where(sub8 == s, 1.0, 0.0)
             pivots = [spread_row(columns[s], s) for columns in diagonals]
             inverses = 1.0 / jnp.where(sub8 == 0, pivots[0], jnp.where(sub8 == 1, pivots[1], pivots[2]))
             for n in range(len(pairs)):
                 columns = diagonals[n]
                 inverse = spread_row(inverses, n)
-                column = jnp.where(row, -1.0, columns[s])
-                line = jnp.where(here, 1.0, spread_row(lines[n], s)) * inverse
-                lines[n] = jnp.where(here | row, 0.0, lines[n]) - column * line
+                column = (columns[s] - unit) * inverse
+                line = jnp.where(here, 1.0, spread_row(lines[n], s))
+                lines[n] = jnp.where(here, unit, lines[n]) - column * line
                 for j in range(s + 1, SUB):
-                    factor = spread_row(columns[j], s) * inverse
-                    columns[j] = jnp.where(row, 0.0, columns[j]) - column * factor
+                    columns[j] = columns[j] - column * spread_row(columns[j], s)
         if turn == LEAF_TURN:
             own_pieces(block)
             own_samples = sample(vectors, tree_lanes, own_rows) if single else samples_ref[:, tree_lanes:]
@@ -394,8 +402,8 @@
             a[turn] = line
 
     inverses = []
-    for a in pairs:
-        both = jnp.concatenate(a, axis=0)
+    for a, scale in zip(pairs, scales):
+        both = jnp.concatenate(a, axis=0) * scale
         inverses.append(split2(jnp.concatenate([jnp.where(low64, both, 0.0), jnp.where(low64, 0.0, both)], axis=0)))
     def times(pair, first, last, parts):
         left = [v[first:last] for v in pair]
@@ -407,8 +415,13 @@
     maps_ref[0, 1] = result[0:half]
     maps_ref[0, 2] = result[half:]
     maps_ref[0, 3] = times(inverses[2], 0, half, (right_maps[3], zero))
+    send(maps_ref.at[:, 1:], maps_out.at[:, 1:])
+    interp_ref[...] = times(inverses[0], 0, half, (right_leaf, wide))
+    send(interp_ref, interp_out)
     maps_ref[0, 0] = times(inverses[0], half, LANES, (zero, right_maps[0]))
-    interp_ref[...] = times(inverses[0], 0, half, (right_leaf, wide))
+    send(maps_ref.at[:, 0:1], maps_out.at[:, 0:1])
+    for copy in copies:
+        copy.wait()
 
 
 def body(row_points, panel_points, test_vectors, leaf_skeleton, node_skeleton):
@@ -430,20 +443,23 @@
     own_rows = rows_here // lax.axis_size("cols")
     lanes = 3 * LANES + own_rows
     block = min(devices, 2**levels * lax.axis_size("cols")) * width
+    outs = (
+        jax.ShapeDtypeStruct((skel, own_rows), jnp.float32),
+        jax.ShapeDtypeStruct((1, levels, skel, 2 * skel), jnp.float32),
+        jax.ShapeDtypeStruct((1, skel, 2 * vec_count), jnp.float32),
+    )
     return pl.pallas_call(
         functools.partial(main_kernel, levels),
-        out_shape=(
-            jax.ShapeDtypeStruct((skel, own_rows), jnp.float32),
-            jax.ShapeDtypeStruct((1, levels, skel, 2 * skel), jnp.float32),
-            jax.ShapeDtypeStruct((1, skel, 2 * vec_count), jnp.float32),
-        ),
+        out_shape=outs,
         in_specs=[VMEM] * 2,
-        out_specs=(VMEM, VMEM, VMEM),
-        scratch_shapes=[
+        out_specs=tuple(pl.BlockSpec(memory_space=pl.ANY) for out in outs),
+        scratch_shapes=[pltpu.VMEM(out.shape, out.dtype) for out in outs]
+        + [
             pltpu.VMEM((block, LANES), jnp.bfloat16),
             pltpu.VMEM((block, lanes), jnp.bfloat16),
             pltpu.VMEM((block, lanes), jnp.bfloat16),
             pltpu.VMEM((2 * vec_count, lanes), jnp.float32),
+            pltpu.SemaphoreType.DMA((4,)),
         ],
     )(pltpu.with_memory_space_constraint(got, pltpu.VMEM), pltpu.with_memory_space_constraint(kept, pltpu.VMEM))
 

time: 23.9 us -> 23.7 us (level)
  no operation moved by 1% of the time
where the time goes in v5:
time: 23.7 us; the launch traced here: 23.5 us
  blocking collectives  16.1 us (68%)
  Pallas kernels  6.79 us (29%)
  between operations  0.64 us (3%)
    all_to_all x1, blocking collectives, body(): got = lax.all_to_all(packed, ('rows', 'cols'), 0, 0, tiled=True)  16.1 us
    pallas_call x1, Pallas kernels, body(): pl.pallas_call(functools.partial(main_kernel, levels), out_shape=outs, in...  5.72 us
    pallas_call x1, Pallas kernels, body(): pl.pallas_call(pack_kernel, out_shape=(pltpu.VMEM((devices, width + SUB,...  1.08 us

profile of v5, /device:TPU:1, one launch (start us, length us, event | category | flops | bytes accessed | tf_op | source)
XLA Modules:
  0.0 23.5 jit_solution(14529046810755267674)
XLA Ops:
  0.6 1.1 %shard_map.76 = (bf16[32,24,128]{2,1,0:T(8,128)(2,1)S(1)}, f32[3,512]{1,0:T(4,128)S(1)}) custom-call(f32[3,512]{1,0:T(4,128)} %rows_ref.1, bf16[3,16]{1,0:T(4,128)(2,1)} %points_ref.1, bf16[16,128]{1,0:T(8,128)(2,1)} %bitcast.1, s32[1,64]{1,0:T(1,128)} %leaf_ref.1, s32[1,4,64]{2,1,0:T(4,128)} %node_ref.1), custom_call_target="tpu_custom_call" | custom-call | tf_op jit(solution)/shard_map/pallas_call | solution.py:432
  1.7 16.1 %all_to_all.5.got_ref = bf16[32,24,128]{2,1,0:T(8,128)(2,1)S(1)} all-to-all(bf16[32,24,128]{2,1,0:T(8,128)(2,1)S(1)} %get-tuple-element.5), channel_id=1, replica_groups=mesh['rows'=16,'cols'=2] {'rows','cols'}, dimensions={0} | all-to-all | bytes 393216 | tf_op jit(solution)/shard_map/all_to_all | solution.py:442
  17.8 5.7 %shard_map.77 = (f32[64,256]{1,0:T(8,128)}, f32[1,4,64,128]{3,2,1,0:T(8,128)}, f32[1,64,256]{2,1,0:T(8,128)}) custom-call(bf16[32,24,128]{2,1,0:T(8,128)(2,1)S(1)} %all_to_all.5.got_ref, f32[3,512]{1,0:T(4,128)S(1)} %get-tuple-element.6.rows_ref), custom_call_target="tpu_custom_call" | custom-call | tf_op jit(solution)/shard_map/pallas_call | solution.py:451

commit v6 on v5

--- a/solution.py
+++ b/solution.py
@@ -16,6 +16,7 @@
 
 LANES = 128
 SUB = 8
+EXTRA = 4
 VMEM = pl.BlockSpec(memory_space=pltpu.VMEM)
 
 TURNS = KAPPA / (2 * math.pi)
@@ -88,17 +89,25 @@
         found = jnp.where(index // LANES == tile, picked, found)
     high, mid, tail = split3(found)
     swapped = swap_halves(s)
-    lines = [
-        jnp.where(low, high[0:1], mid[0:1]),
-        jnp.where(low, tail[0:1], high[1:2]),
-        jnp.where(low, mid[1:2], tail[1:2]),
-        jnp.where(low, high[2:3], mid[2:3]),
-        tail[2:3],
-        jnp.where(low, s[1:2], swapped[2:3]),
-        jnp.where(low, s[3:4], swapped[4:5]),
-        s[5:6] + pltpu.roll(s, width, axis=1)[6:7] + pltpu.roll(s, 2 * width, axis=1)[7:8],
-    ]
+    points = s[5:6] + pltpu.roll(s, width, axis=1)[6:7] + pltpu.roll(s, 2 * width, axis=1)[7:8]
+    halves = (
+        [
+            jnp.where(low, high[0:1], mid[0:1]),
+            jnp.where(low, tail[0:1], high[1:2]),
+            jnp.where(low, mid[1:2], tail[1:2]),
+        ],
+        [
+            jnp.where(low, high[2:3], mid[2:3]),
+            jnp.where(low, s[1:2], swapped[2:3]),
+            jnp.where(low, s[3:4], swapped[4:5]),
+        ],
+    )
+    column = lax.axis_index("cols")
+    lines = [jnp.where(column == 0, a, b) for a, b in zip(*halves)]
+    lines.append(jnp.where(low, points, tail[2:3]))
     block = jnp.concatenate([vectors_ref[...].astype(jnp.float32)] + lines, axis=0).astype(jnp.bfloat16)
+
+    block = block.reshape(out_ref.shape[1:])
 
     def put(device, unused):
         out_ref[device] = block
@@ -139,7 +148,7 @@
     group_leaves = 2**levels
     group_devices = group_leaves * cols
     devices = got_ref.shape[0]
-    width = got_ref.shape[1] - SUB
+    width = (got_ref.shape[1] - 1) * EXTRA
     width_bits = width.bit_length() - 1
     lane8 = iota((SUB, LANES), 1)
     sub8 = iota((SUB, LANES), 0)
@@ -168,7 +177,7 @@
     block_devices = min(devices, group_devices)
     single = block_devices == devices
     block = block_devices * width
-    vec_count = got_ref.shape[2]
+    vec_count = got_ref.shape[-1]
     eye = (iota((vec_count, vec_count), 0) == iota((vec_count, vec_count), 1)).astype(jnp.bfloat16)
     shape = (width, LANES)
     lane_of = iota(shape, 1)
@@ -182,13 +191,13 @@
     )
 
     def panel_vectors(number):
-        got = got_ref[pl.ds(number * block_devices, block_devices), 0:width, :].astype(jnp.float32)
+        got = got_ref[pl.ds(number * block_devices, block_devices), 0 : width // EXTRA].astype(jnp.float32)
         vectors = got.reshape(block, vec_count).astype(jnp.bfloat16)
         return mm(eye, vectors, dims=((1,), (1,))).astype(jnp.bfloat16)
 
     def panel_left(number):
-        tail = got_ref[pl.ds(number * block_devices, block_devices), width : width + SUB, :].astype(jnp.float32)
-        points = [jnp.where(keep, jnp.broadcast_to(tail[d, SUB - 1 : SUB], keep.shape), 0.0) for d in range(block_devices)]
+        tail = got_ref[pl.ds(number * block_devices, block_devices), width // EXTRA].astype(jnp.float32)
+        points = [jnp.where(keep, jnp.broadcast_to(tail[d, EXTRA - 1 : EXTRA], keep.shape), 0.0) for d in range(block_devices)]
         points = jnp.concatenate(points, axis=0)
         high, low = split2(points * points)
         left = mm(jnp.concatenate([points.astype(jnp.bfloat16), high, low], axis=1), collect) + ones
@@ -214,11 +223,13 @@
 
     vectors = panel_vectors(0)
     group_start = (leaf // group_leaves) * group_devices
-    extra = got_ref[pl.ds(group_start, group_devices), width : width + SUB, :].astype(jnp.float32)
-    extra = extra.reshape(group_devices * SUB, LANES).astype(jnp.bfloat16)
-    shape = (7 * 16, group_devices * SUB)
+    extra = got_ref[pl.ds(group_start, group_devices), width // EXTRA].astype(jnp.float32)
+    extra = extra.reshape(group_devices * EXTRA, LANES).astype(jnp.bfloat16)
+    shape = (7 * 16, group_devices * EXTRA)
     at = iota(shape, 0)
-    source = ((at & 7) * 2 + ((at >> 3) & 1)) * (cols * SUB) + (at >> 4)
+    line = at >> 4
+    place = jnp.where(line < 3, line, jnp.where(line == 3, EXTRA, jnp.where(line == 4, EXTRA - 1, line)))
+    source = ((at & 7) * 2 + ((at >> 3) & 1)) * (cols * EXTRA) + place
     picked = mm((iota(shape, 1) == source).astype(jnp.bfloat16), extra)
     even = [picked[r * 16 : r * 16 + 8] for r in range(7)]
     odd = [picked[r * 16 + 8 : r * 16 + 16] for r in range(7)]
@@ -227,7 +238,7 @@
     coords = [
         jnp.where(low8, even[0] + even_s[0] + even[1], odd[0] + odd_s[0] + odd_s[1]),
         jnp.where(low8, even_s[1] + (even[2] + even_s[2]), odd[1] + (odd[2] + odd_s[2])),
-        jnp.where(low8, even[3] + even_s[3] + even[4], odd[3] + odd_s[3] + odd[4]),
+        jnp.where(low8, even[3] + even_s[3] + even_s[4], odd[3] + odd_s[3] + odd[4]),
     ]
     lists = [
         jnp.where(low8, even[5], even_s[5]).astype(jnp.int32),
@@ -432,7 +443,7 @@
     packed, kept = pl.pallas_call(
         pack_kernel,
         out_shape=(
-            pltpu.VMEM((devices, width + SUB, vec_count), jnp.bfloat16),
+            pltpu.VMEM((devices, width // EXTRA + 1, EXTRA, vec_count), jnp.bfloat16),
             pltpu.VMEM(row_points.shape, jnp.float32),
         ),
         in_specs=[VMEM] * 5,

time: 23.7 us -> 23.5 us (level); the launches traced: 23.5 us -> 23.1 us
  blocking collectives: 16.1 us -> 15.6 us
    all_to_all x1, blocking collectives: 16.1 us -> 15.6 us  [body(): got = lax.all_to_all(packed, ('rows', 'cols'), 0, 0, tiled=True)]
where the time goes in v6:
time: 23.5 us; the launch traced here: 23.1 us
  blocking collectives  15.6 us (66%)
  Pallas kernels  6.87 us (29%)
  between operations  0.64 us (3%)
    all_to_all x1, blocking collectives, body(): got = lax.all_to_all(packed, ('rows', 'cols'), 0, 0, tiled=True)  15.6 us
    pallas_call x1, Pallas kernels, body(): pl.pallas_call(functools.partial(main_kernel, levels), out_shape=outs, in...  5.76 us
    pallas_call x1, Pallas kernels, body(): pl.pallas_call(pack_kernel, out_shape=(pltpu.VMEM((devices, width // EXTR...  1.12 us

profile of v6, /device:TPU:1, one launch (start us, length us, event | category | flops | bytes accessed | tf_op | source)
XLA Modules:
  0.0 23.1 jit_solution(5705210986286682603)
XLA Ops:
  0.6 1.1 %shard_map.76 = (bf16[32,5,4,128]{3,2,1,0:T(4,128)(2,1)S(1)}, f32[3,512]{1,0:T(4,128)S(1)}) custom-call(f32[3,512]{1,0:T(4,128)} %rows_ref.1, bf16[3,16]{1,0:T(4,128)(2,1)} %points_ref.1, bf16[16,128]{1,0:T(8,128)(2,1)} %bitcast.1, s32[1,64]{1,0:T(1,128)} %leaf_ref.1, s32[1,4,64]{2,1,0:T(4,128)} %node_ref.1), custom_call_target="tpu_custom_call" | custom-call | tf_op jit(solution)/shard_map/pallas_call | solution.py:443
  1.8 15.6 %all_to_all.5.got_ref = bf16[32,5,4,128]{3,2,1,0:T(4,128)(2,1)S(1)} all-to-all(bf16[32,5,4,128]{3,2,1,0:T(4,128)(2,1)S(1)} %get-tuple-element.5), channel_id=1, replica_groups=mesh['rows'=16,'cols'=2] {'rows','cols'}, dimensions={0} | all-to-all | bytes 327680 | tf_op jit(solution)/shard_map/all_to_all | solution.py:453
  17.3 5.8 %shard_map.77 = (f32[64,256]{1,0:T(8,128)}, f32[1,4,64,128]{3,2,1,0:T(8,128)}, f32[1,64,256]{2,1,0:T(8,128)}) custom-call(bf16[32,5,4,128]{3,2,1,0:T(4,128)(2,1)S(1)} %all_to_all.5.got_ref, f32[3,512]{1,0:T(4,128)S(1)} %get-tuple-element.6.rows_ref), custom_call_target="tpu_custom_call" | custom-call | tf_op jit(solution)/shard_map/pallas_call | solution.py:462

commit v7 on v6

--- a/solution.py
+++ b/solution.py
@@ -57,8 +57,9 @@
 
 
 def mm_split(a, b):
-    (a_high, a_low), (b_high, b_low) = a, b
-    return mm(jnp.concatenate([a_high, a_high, a_low], axis=1), jnp.concatenate([b_high, b_low, b_high], axis=0))
+    rows, lanes = a[0].shape[0], b[0].shape[1]
+    out = mm(jnp.concatenate(a, axis=0), jnp.concatenate(b, axis=1))
+    return out[:rows, :lanes] + (out[:rows, lanes:] + out[rows:, :lanes])
 
 
 def split3(x):
@@ -116,8 +117,7 @@
     lax.fori_loop(0, out_ref.shape[0], put, 0)
 
 
-SETUP_PIECES = 4
-STAGE_PIECES = 4
+STAGE_PIECES = 8
 TURN_PIECES = (0, 0, 0, 0, 0, 0, 0, 0)
 LEAF_TURN = 3
 
@@ -212,16 +212,6 @@
         both = [mm(vectors, k[:, lane : lane + lanes]) for k in (kre_ref, kim_ref)]
         return jnp.concatenate(both, axis=0)
 
-    chunk = min(LANES, block)
-    panel_left(0)
-    right_own = right_side([own_points[c : c + 1] for c in range(3)])
-    pieces = list(range(0, block, 16)) if single else []
-
-    def own_pieces(count):
-        for unused in range(min(count, len(pieces))):
-            fill(pieces.pop(0), 16, right_own, tree_lanes)
-
-    vectors = panel_vectors(0)
     group_start = (leaf // group_leaves) * group_devices
     extra = got_ref[pl.ds(group_start, group_devices), width // EXTRA].astype(jnp.float32)
     extra = extra.reshape(group_devices * EXTRA, LANES).astype(jnp.bfloat16)
@@ -261,11 +251,20 @@
         siblings.append([own_row(v) for v in other])
         stacked = [jnp.where(low8 == upper, b, a) for a, b in zip(own, other)]
         own_lists.append(own_row(lists[level]))
-        own_pieces(SETUP_PIECES)
     low1 = iota((1, LANES), 1) < half
     tiles = [[own_row(v) for v in coords]]
     tiles.append([jnp.where(low1, a, b) for a, b in zip(siblings[0], siblings[1])])
     tiles.append(siblings[2])
+    chunk = min(LANES, block)
+    panel_left(0)
+    right_own = right_side([own_points[c : c + 1] for c in range(3)])
+    pieces = list(range(0, block, 16)) if single else []
+
+    def own_pieces(count):
+        for unused in range(min(count, len(pieces))):
+            fill(pieces.pop(0), 16, right_own, tree_lanes)
+
+    vectors = panel_vectors(0)
     right_tree = jnp.concatenate([right_side(t) for t in tiles], axis=1)
 
     for at in range(0, block, chunk):
@@ -407,7 +406,8 @@
 
             high = line.astype(jnp.bfloat16).astype(jnp.float32)
             right = placed(high), placed(line - high)
-            product = mm_split(split2(jnp.concatenate([a[b] for b in others], axis=0)), right)
+            padded = others + [turn] * (len(others) % 2)
+            product = mm_split(split2(jnp.concatenate([a[b] for b in padded], axis=0)), right)
             for number, b in enumerate(others):
                 a[b] = cleared[b] - product[number * SUB : (number + 1) * SUB]
             a[turn] = line

time: 23.5 us -> 23.3 us (level)
  no operation moved by 1% of the time
where the time goes in v7:
time: 23.3 us; the launch traced here: 22.9 us
  blocking collectives  15.6 us (67%)
  Pallas kernels  6.69 us (29%)
  between operations  0.64 us (3%)
    all_to_all x1, blocking collectives, body(): got = lax.all_to_all(packed, ('rows', 'cols'), 0, 0, tiled=True)  15.6 us
    pallas_call x1, Pallas kernels, body(): pl.pallas_call(functools.partial(main_kernel, levels), out_shape=outs, in...  5.58 us
    pallas_call x1, Pallas kernels, body(): pl.pallas_call(pack_kernel, out_shape=(pltpu.VMEM((devices, width // EXTR...  1.12 us

profile of v7, /device:TPU:1, one launch (start us, length us, event | category | flops | bytes accessed | tf_op | source)
XLA Modules:
  0.0 22.9 jit_solution(10943268012885268891)
XLA Ops:
  0.6 1.1 %shard_map.76 = (bf16[32,5,4,128]{3,2,1,0:T(4,128)(2,1)S(1)}, f32[3,512]{1,0:T(4,128)S(1)}) custom-call(f32[3,512]{1,0:T(4,128)} %rows_ref.1, bf16[3,16]{1,0:T(4,128)(2,1)} %points_ref.1, bf16[16,128]{1,0:T(8,128)(2,1)} %bitcast.1, s32[1,64]{1,0:T(1,128)} %leaf_ref.1, s32[1,4,64]{2,1,0:T(4,128)} %node_ref.1), custom_call_target="tpu_custom_call" | custom-call | tf_op jit(solution)/shard_map/pallas_call | solution.py:443
  1.8 15.6 %all_to_all.5.got_ref = bf16[32,5,4,128]{3,2,1,0:T(4,128)(2,1)S(1)} all-to-all(bf16[32,5,4,128]{3,2,1,0:T(4,128)(2,1)S(1)} %get-tuple-element.5), channel_id=1, replica_groups=mesh['rows'=16,'cols'=2] {'rows','cols'}, dimensions={0} | all-to-all | bytes 327680 | tf_op jit(solution)/shard_map/all_to_all | solution.py:453
  17.3 5.6 %shard_map.77 = (f32[64,256]{1,0:T(8,128)}, f32[1,4,64,128]{3,2,1,0:T(8,128)}, f32[1,64,256]{2,1,0:T(8,128)}) custom-call(bf16[32,5,4,128]{3,2,1,0:T(4,128)(2,1)S(1)} %all_to_all.5.got_ref, f32[3,512]{1,0:T(4,128)S(1)} %get-tuple-element.6.rows_ref), custom_call_target="tpu_custom_call" | custom-call | tf_op jit(solution)/shard_map/pallas_call | solution.py:462

commit v8 on v7

--- a/solution.py
+++ b/solution.py
@@ -114,7 +114,7 @@
         out_ref[device] = block
         return unused
 
-    lax.fori_loop(0, out_ref.shape[0], put, 0)
+    lax.fori_loop(0, out_ref.shape[0], put, 0, unroll=8)
 
 
 STAGE_PIECES = 8

time: 23.3 us -> 23.1 us (level)
  no operation moved by 1% of the time
where the time goes in v8:
time: 23.1 us; the launch traced here: 22.8 us
  blocking collectives  15.6 us (68%)
  Pallas kernels  6.56 us (28%)
  between operations  0.64 us (3%)
    all_to_all x1, blocking collectives, body(): got = lax.all_to_all(packed, ('rows', 'cols'), 0, 0, tiled=True)  15.6 us
    pallas_call x1, Pallas kernels, body(): pl.pallas_call(functools.partial(main_kernel, levels), out_shape=outs, in...  5.58 us
    pallas_call x1, Pallas kernels, body(): pl.pallas_call(pack_kernel, out_shape=(pltpu.VMEM((devices, width // EXTR...  0.98 us

profile of v8, /device:TPU:1, one launch (start us, length us, event | category | flops | bytes accessed | tf_op | source)
XLA Modules:
  0.0 22.8 jit_solution(9692117471022075139)
XLA Ops:
  0.6 1.0 %shard_map.76 = (bf16[32,5,4,128]{3,2,1,0:T(4,128)(2,1)S(1)}, f32[3,512]{1,0:T(4,128)S(1)}) custom-call(f32[3,512]{1,0:T(4,128)} %rows_ref.1, bf16[3,16]{1,0:T(4,128)(2,1)} %points_ref.1, bf16[16,128]{1,0:T(8,128)(2,1)} %bitcast.1, s32[1,64]{1,0:T(1,128)} %leaf_ref.1, s32[1,4,64]{2,1,0:T(4,128)} %node_ref.1), custom_call_target="tpu_custom_call" | custom-call | tf_op jit(solution)/shard_map/pallas_call | solution.py:443
  1.6 15.6 %all_to_all.5.got_ref = bf16[32,5,4,128]{3,2,1,0:T(4,128)(2,1)S(1)} all-to-all(bf16[32,5,4,128]{3,2,1,0:T(4,128)(2,1)S(1)} %get-tuple-element.5), channel_id=1, replica_groups=mesh['rows'=16,'cols'=2] {'rows','cols'}, dimensions={0} | all-to-all | bytes 327680 | tf_op jit(solution)/shard_map/all_to_all | solution.py:453
  17.2 5.6 %shard_map.77 = (f32[64,256]{1,0:T(8,128)}, f32[1,4,64,128]{3,2,1,0:T(8,128)}, f32[1,64,256]{2,1,0:T(8,128)}) custom-call(bf16[32,5,4,128]{3,2,1,0:T(4,128)(2,1)S(1)} %all_to_all.5.got_ref, f32[3,512]{1,0:T(4,128)S(1)} %get-tuple-element.6.rows_ref), custom_call_target="tpu_custom_call" | custom-call | tf_op jit(solution)/shard_map/pallas_call | solution.py:462
